TPU v7x, 32 devices: a whole 2x2x4 slice. The times are simulated.
32 devices in a mesh: slide: 4 (over y, x), seq: 8 (over z, core).
Axes of the slice: x: 2, y: 2, z: 4, core: 2. Of those that a mesh axis runs over, the one named last changes fastest.
Arguments:
- embeds: bfloat16 [12288, 1536], P(('slide', 'seq'))
- destination: int32 [12288, 1], P(('slide', 'seq')), may hold values from 0 to 31; in each aligned block of 384 rows (0 to 383, 384 to 767, ...) at most 24 rows name the same one
- norm_gain: float32 [1536], replicated, may hold values from 0.1 to 1.9
- qkv_weight: bfloat16 [1536, 4608], replicated
- out_weight: bfloat16 [1536, 1536], replicated, may hold values from -0.15625 to 0.15625
- finding_queries: bfloat16 [256, 1536], replicated
Outputs:
- layer_out: bfloat16 [24576, 1536], P(('slide', 'seq'))
- heatmap: float32 [24576, 256], P(('slide', 'seq'))
Inputs may be any that keep to these rules, and one draw needn't show every extreme that they name: `destination`: each block of 384 rows (one encoder device) names any one device at most 24 times, and some block names some device exactly 24 times; every device is named by some row.
All inputs are finite; a program needn't handle non-finite values.
Results may differ from a plain program's by a relative error of at most 0.01225.
The roundings to bfloat16 on the way count: a program that leaves them out, or rounds other values in their place, can miss the bound.
Values may be sent and summed in bfloat16 or wider, within the bound.
A program may use at most 192 MiB of HBM per device.

v0:
```python
import jax
import jax.numpy as jnp
from jax import lax
from jax.sharding import PartitionSpec as P

HEADS = 12


MASKED = -1e30
EPSILON = 1e-06


def partner_2(value, axis, bit):
    mask = 2**bit
    pairs = [(source, source ^ mask) for source in range(lax.axis_size(axis))]
    return lax.ppermute(value, axis, pairs)


def select(rows, rate, spread):
    count = rows.shape[0]
    heads = rows.shape[1]
    trailing = rows.shape[2:]
    grouped = rows.reshape((count // rate, rate, heads // (rate * spread), rate, spread) + trailing)
    picked = jnp.stack([grouped[:, phase, :, phase] for phase in range(rate)], axis=2)
    return picked.reshape((count // rate, heads) + trailing)


def spread_back(rows, rate, fill):
    count = rows.shape[0]
    heads = rows.shape[1]
    trailing = rows.shape[2:]
    chosen = (jnp.arange(rate)[:, None] == jnp.arange(heads)[None, :] % rate).reshape(
        (1, rate, heads) + (1,) * len(trailing)
    )
    widened = jnp.where(chosen, rows[:, None], jnp.asarray(fill, rows.dtype))
    return widened.reshape((count * rate, heads) + trailing)


def join_rows(mine, theirs):
    return tuple(
        (jnp.concatenate([own_part, far_part], axis=0) for own_part, far_part in zip(mine, theirs))
    )


def attend(query, key_rows, value, presence):
    scale = query.shape[-1] ** (-0.5)
    phases = presence.shape[1]
    allowed = (jnp.tile(presence, (1, query.shape[1] // phases)) > 0.5).T[:, None, :]
    scores = jnp.einsum("qhe,khe->hqk", query, key_rows, preferred_element_type=jnp.float32) * scale
    scores = jnp.where(allowed, scores, MASKED)
    peak = jnp.max(scores, axis=2, keepdims=True)
    exp_scores = jnp.where(allowed, jnp.exp(scores - peak), 0.0)
    total = jnp.sum(exp_scores, axis=2)
    weighted = jnp.einsum(
        "hqk,khe->qhe", exp_scores.astype(jnp.bfloat16), value, preferred_element_type=jnp.float32
    )
    bounded = jnp.maximum(total, 1.0)
    result = weighted / bounded.T[:, :, None]
    log_total = jnp.where(total > 0.0, peak[:, :, 0] + jnp.log(bounded), MASKED).T
    return (result, log_total)


def merge_totals(first, second):
    peak = jnp.maximum(first[0], second[0])
    return (peak, first[1] * jnp.exp(first[0] - peak) + second[1] * jnp.exp(second[0] - peak))


def shards(embeds, destination, norm_gain, qkv_weight, out_weight, finding_queries):
    devices = lax.axis_size(("slide", "seq"))
    seq_count = lax.axis_size("seq")
    slots = embeds.shape[0] * 2
    capacity = slots // devices
    width = embeds.shape[1]
    heads = HEADS
    head_size = width // heads
    target = destination[:, 0]
    one_hot = (target[:, None] == jnp.arange(devices, dtype=jnp.int32)[None, :]).astype(jnp.int32)
    rank = jnp.sum(jnp.cumsum(one_hot, axis=0) * one_hot, axis=1) - 1
    place = target * capacity + rank
    buffer = jnp.zeros((devices * capacity, width), jnp.bfloat16).at[place].set(embeds)
    flags = jnp.zeros((devices * capacity,), jnp.int32).at[place].set(1)
    tiles, valid = (
        lax.all_to_all(buffer, ("slide", "seq"), split_axis=0, concat_axis=0, tiled=True),
        lax.all_to_all(flags, ("slide", "seq"), split_axis=0, concat_axis=0, tiled=True),
    )
    tile_f32 = tiles.astype(jnp.float32)
    normed = (
        tile_f32
        * lax.rsqrt(jnp.mean(tile_f32 * tile_f32, axis=1, keepdims=True) + EPSILON)
        * norm_gain
    ).astype(jnp.bfloat16)
    projected = jnp.dot(normed, qkv_weight, preferred_element_type=jnp.float32).astype(jnp.bfloat16)
    projected = projected.reshape(slots, 3, heads, head_size)
    query, key_rows, value = (projected[:, 0], projected[:, 1], projected[:, 2])
    presence = valid.astype(jnp.bfloat16)
    out_one, log_one = attend(query, key_rows, value, presence.reshape(slots, 1))
    near = (select(key_rows, 2, 1), select(value, 2, 1), presence.reshape(slots // 2, 2))
    partner = partner_2((near[0], near[1], near[2]), "seq", 0)
    pair_all = join_rows(near, partner)
    out_two, log_two = attend(select(query, 2, 1), pair_all[0], pair_all[1], pair_all[2])
    group = (select(key_rows, 4, 1), select(value, 4, 1), presence.reshape(slots // 4, 4))
    for bit_level in (0, 1):
        other = partner_2((group[0], group[1], group[2]), "seq", bit_level)
        group = join_rows(group, other)
    out_four, log_four = attend(select(query, 4, 1), group[0], group[1], group[2])
    results = (out_one, spread_back(out_two, 2, 0.0), spread_back(out_four, 4, 0.0))
    stacked = jnp.stack(
        [log_one, spread_back(log_two, 2, MASKED), spread_back(log_four, 4, MASKED)]
    )
    top = jnp.max(stacked, axis=0)
    factors = jnp.exp(stacked - top)[..., None]
    mixed = (factors[0] * results[0] + factors[1] * results[1] + factors[2] * results[2]) / jnp.sum(
        factors, axis=0
    )
    mixed = mixed.astype(jnp.bfloat16).reshape(slots, width)
    layer_out = (tile_f32 + jnp.dot(mixed, out_weight, preferred_element_type=jnp.float32)).astype(
        jnp.bfloat16
    )
    out_f32 = layer_out.astype(jnp.float32)
    keys_find = (
        out_f32 * lax.rsqrt(jnp.mean(out_f32 * out_f32, axis=1, keepdims=True) + EPSILON)
    ).astype(jnp.bfloat16)
    keys_find = keys_find.reshape(slots, heads, head_size)
    queries_find = finding_queries.reshape(finding_queries.shape[0], heads, head_size)
    scores = jnp.einsum(
        "fhe,the->hft", queries_find, keys_find, preferred_element_type=jnp.float32
    ) * head_size ** (-0.5)
    allowed = (valid > 0)[None, None, :]
    scores = jnp.where(allowed, scores, MASKED)
    peak_local = jnp.max(scores, axis=2)
    exp_scores = jnp.where(allowed, jnp.exp(scores - peak_local[:, :, None]), 0.0)
    total_local = jnp.sum(exp_scores, axis=2)
    peak_all, total_all = (peak_local, total_local)
    for bit_level in range(seq_count.bit_length() - 1):
        other_peak, other_total = partner_2((peak_all, total_all), "seq", bit_level)
        peak_all, total_all = merge_totals((peak_all, total_all), (other_peak, other_total))
    probs = exp_scores * (jnp.exp(peak_local - peak_all) / total_all)[:, :, None]
    heat = jnp.sum(probs, axis=0).T * (seq_count * slots / heads)
    return (layer_out, heat)


def solution(mesh):
    in_specs = (P(("slide", "seq"), None), P(("slide", "seq"), None), P(), P(), P(), P())
    out_specs = (P(("slide", "seq"), None), P(("slide", "seq"), None))
    return jax.shard_map(shards, mesh=mesh, in_specs=in_specs, out_specs=out_specs, check_vma=False)
```

profile of v0, /device:TPU:0, one launch (start us, length us, event | category | flops | bytes accessed | tf_op | source)
XLA Modules:
  0.0 306.6 jit_solution(6708858079010389491)
XLA Ops:
  3.3 2.9 scatter_custom_fusion.1
  6.9 7.3 %all-to-all-start.1 = ((s32[32,24,1]{1,2,0:T(1,128)}), s32[32,24,1]{1,2,0:T(1,128)S(1)}, u32[]{:S(2)}, u32[]{:S(2)}) async-start(s32[32,24,1]{1,2,0:T(1,128)} %bitcast.3), calls=%async_computation.1 | async-start | bytes 32768 | tf_op jit(solution)/shard_map/all_to_all | solution.py:84
  14.2 4.8 %scatter_custom_fusion = bf16[768,1536]{1,0:T(8,128)(2,1)} fusion(s32[384]{0:T(512)S(1)} %fusion.78, bf16[384,1536]{1,0:T(8,128)(2,1)} %param.6, bf16[]{:T(256)} %constant.60.clone.1), kind=kCustom, calls=%fused_computation.77 | custom fusion | bytes 2359808 | tf_op jit(solution)/shard_map/scatter | solution.py:80
  19.1 2.2 all-to-all-done.1
  21.3 3.9 %all-to-all-start = ((bf16[32,24,1536]{2,1,0:T(8,128)(2,1)}), bf16[32,24,1536]{2,1,0:T(8,128)(2,1)S(1)}, u32[]{:S(2)}, u32[]{:S(2)}) async-start(bf16[32,24,1536]{2,1,0:T(8,128)(2,1)} %bitcast.227), calls=%async_computation | async-start | bytes 4718592 | tf_op jit(solution)/shard_map/all_to_all | solution.py:83
  29.7 1.9 collective-permute-start.3
  32.4 31.8 %collective-permute-done.3 = bf16[384,4]{0,1:T(4,128)(2,1)S(1)} collective-permute-done((bf16[384,4]{0,1:T(4,128)(2,1)S(1)}, bf16[384,4]{0,1:T(4,128)(2,1)S(1)}, u32[]{:S(2)}, u32[]{:S(2)}) %collective-permute-start.3) | collective-permute-done | bytes 3104 | tf_op jit(solution)/shard_map/ppermute | solution.py:16
  64.9 16.1 %all-to-all-done = bf16[32,24,1536]{2,1,0:T(8,128)(2,1)S(1)} async-done(((bf16[32,24,1536]{2,1,0:T(8,128)(2,1)}), bf16[32,24,1536]{2,1,0:T(8,128)(2,1)S(1)}, u32[]{:S(2)}, u32[]{:S(2)}) %all-to-all-start) | async-done | bytes 2359328 | tf_op jit(solution)/shard_map/all_to_all | solution.py:83
  82.2 16.1 %convolution_convert_fusion = bf16[768,4608]{1,0:T(8,128)(2,1)} fusion(bf16[768,1536]{1,0:T(8,128)(2,1)S(1)} %fusion.26, bf16[1536,4608]{1,0:T(8,128)(2,1)} %param.9), kind=kOutput, calls=%fused_computation.20 | convolution fusion | flops 10875174912 | bytes 23592960 | tf_op jit(solution)/shard_map/dot_general | solution.py:92
  98.4 10.3 %copy.200 = bf16[768,4608]{0,1:T(8,128)(2,1)} copy(bf16[768,4608]{1,0:T(8,128)(2,1)} %convolution_convert_fusion) | data formatting | bytes 14155776 | tf_op jit(solution)/shard_map/convert_element_type | solution.py:92
  108.7 6.5 %fusion.101 = (bf16[768,1,12,128]{0,3,2,1:T(8,128)(2,1)}, bf16[768,1,12,128]{0,3,2,1:T(8,128)(2,1)}, bf16[768,1,12,128]{0,3,2,1:T(8,128)(2,1)}) fusion(bf16[768,3,12,128]{0,3,2,1:T(8,128)(2,1)} %bitcast.215), kind=kLoop, calls=%fused_computation.170 | loop fusion | bytes 14155776 | tf_op jit(solution)/shard_map/slice | solution.py:94
  115.5 12.4 %fusion = (f32[12,768]{1,0:T(8,128)S(1)}, f32[12,768,768]{1,2,0:T(8,128)}) fusion(pred[768]{0:T(1024)(128)(4,1)S(1)} %gt.67, bf16[768,3,12,128]{0,3,2,1:T(8,128)(2,1)S(1)} %bitcast.216), kind=kOutput, calls=%fused_computation.4 | convolution fusion | flops 1833163776 | bytes 33068032 | tf_op jit(solution)/shard_map/qhe,khe->hqk/dot_general | solution.py:49
  127.9 15.1 %fusion.3 = f32[12,128,768]{2,1,0:T(8,128)} fusion(f32[12,768,768]{1,2,0:T(8,128)} %get-tuple-element.40, f32[12,768]{1,0:T(8,128)S(1)} %get-tuple-element.39, pred[768]{0:T(1024)(128)(4,1)S(1)} %gt.67, bf16[768,3,12,128]{0,3,2,1:T(8,128)(2,1)S(1)} %bitcast.217), kind=kOutput, calls=%fused_computation.9 | convolution fusion | flops 1847328768 | bytes 35439616 | tf_op jit(solution)/shard_map/hqk,khe->qhe/dot_general | solution.py:54
  143.0 13.2 %fusion.2 = f32[12,768]{1,0:T(8,128)S(1)} fusion(f32[12,768,768]{1,2,0:T(8,128)} %get-tuple-element.40, f32[12,768]{1,0:T(8,128)S(1)} %get-tuple-element.39, pred[768]{0:T(1024)(128)(4,1)S(1)} %gt.67), kind=kLoop, calls=%fused_computation.6 | loop fusion | flops 35380224 | bytes 28386048 | tf_op jit(solution)/shard_map/reduce_sum | solution.py:53
  156.2 3.0 copy.231
  161.5 4.3 %copy.257 = bf16[768,1,12,128]{3,0,2,1:T(8,128)(2,1)} copy(bf16[768,1,12,128]{0,3,2,1:T(8,128)(2,1)} %get-tuple-element.9) | data formatting | bytes 4718592
  165.8 3.6 %fusion.106 = (bf16[192,1,3,1,1,128]{5,1,0,3,2,4:T(2,128)(2,1)}, bf16[192,1,3,1,1,128]{5,1,0,3,2,4:T(2,128)(2,1)S(1)}, bf16[192,1,3,1,1,128]{5,1,0,3,2,4:T(2,128)(2,1)}, bf16[192,1,3,1,1,128]{5,1,0,3,2,4:T(2,128)(2,1)}) fusion(bf16[192,4,3,4,1,128]{5,1,0,3,2,4:T(4,128)(2,1)} %bitcast.222), kind=kLoop, calls=%fused_computation.175 | loop fusion | bytes 1179648 | tf_op jit(solution)/shard_map/slice | solution.py:24
  169.3 4.4 %copy.258 = bf16[768,1,12,128]{3,0,2,1:T(8,128)(2,1)} copy(bf16[768,1,12,128]{0,3,2,1:T(8,128)(2,1)} %get-tuple-element.8) | data formatting | bytes 4718592
  173.8 3.0 fusion.105
  178.3 2.2 fusion.104
  180.5 2.2 fusion.103
  184.0 2.2 fusion.102
  191.4 1.8 pad_maximum_fusion.5
  193.3 2.4 pad_maximum_fusion.4
  195.7 2.4 pad_maximum_fusion.2
  198.1 2.0 collective-permute-start.5
  200.1 3.8 %fusion.6 = (f32[12,384]{1,0:T(8,128)S(1)}, f32[12,384,768]{2,1,0:T(8,128)S(1)}) fusion(pred[12,768]{1,0:T(8,128)(4,1)S(1)} %bitcast.249, bf16[384,12,128]{2,0,1:T(8,128)(2,1)S(1)} %bitcast.242, bf16[384,12,128]{2,0,1:T(8,128)(2,1)} %collective-permute-done.1, bf16[384,12,128]{2,0,1:T(8,128)(2,1)} %bitcast.19), kind=kOutput, calls=%fused_computation.11 | convolution fusion | flops 921300480 | bytes 17722368 | tf_op jit(solution)/shard_map/qhe,khe->hqk/dot_general | solution.py:49
  203.9 4.3 %fusion.8 = f32[12,384]{1,0:T(8,128)S(1)} fusion(f32[12,384,768]{2,1,0:T(8,128)S(1)} %get-tuple-element.38, f32[12,384]{1,0:T(8,128)S(1)} %get-tuple-element.37, pred[12,768]{1,0:T(8,128)(4,1)S(1)} %bitcast.250), kind=kLoop, calls=%fused_computation.13 | loop fusion | flops 17690112 | bytes 14201856 | tf_op jit(solution)/shard_map/reduce_sum | solution.py:53
  208.2 5.1 %bitcast_divide_fusion.1 = f32[384,12,128]{0,2,1:T(8,128)} fusion(f32[384,12]{0,1:T(8,128)S(1)} %maximum_bitcast_fusion.1, f32[12,384,768]{2,1,0:T(8,128)S(1)} %get-tuple-element.38, f32[12,384]{1,0:T(8,128)S(1)} %get-tuple-element.37, pred[12,768]{1,0:T(8,128)(4,1)S(1)} %bitcast.251, bf16[384,12,128]{0,2,1:T(8,128)(2,1)S(1)} %collective-permute-done.6, ...), kind=kOutput, calls=%fused_computation.69 | convolution fusion | flops 928972800 | bytes 18920448 | tf_op jit(solution)/shard_map/hqk,khe->qhe/dot_general | solution.py:54
  213.3 2.0 copy.233
  215.3 3.8 %broadcast_in_dim.247 = f32[384,2,12,128]{3,1,0,2:T(2,128)} broadcast(f32[384,12,128]{2,0,1:T(8,128)S(1)} %copy.233), dimensions={0,2,3} | broadcast | bytes 7077888 | tf_op jit(solution)/shard_map/jit(_where)/broadcast_in_dim | solution.py:35
  219.1 6.1 %copy.234 = f32[768,12,128]{0,2,1:T(8,128)} copy(f32[768,12,128]{2,0,1:T(8,128)} %bitcast.218) | data formatting | bytes 9437184 | tf_op jit(solution)/shard_map/jit(_where)/broadcast_in_dim | solution.py:35
  226.2 23.0 %collective-permute-done.5 = bf16[384,12,128]{2,0,1:T(8,128)(2,1)} collective-permute-done((bf16[384,12,128]{2,0,1:T(8,128)(2,1)}, bf16[384,12,128]{2,0,1:T(8,128)(2,1)}, u32[]{:S(2)}, u32[]{:S(2)}) %collective-permute-start.5) | collective-permute-done | bytes 1179680 | tf_op jit(solution)/shard_map/ppermute | solution.py:16
  249.2 2.8 fusion.15
  252.0 2.3 fusion.17
  254.3 3.9 %fusion.61 = f32[192,12,128]{2,0,1:T(8,128)S(1)} fusion(bf16[384,12,128]{2,0,1:T(8,128)(2,1)} %collective-permute-done.8, bf16[192,12,128]{2,0,1:T(8,128)(2,1)} %collective-permute-done.7, bf16[192,12,128]{2,0,1:T(8,128)(2,1)} %bitcast.54, f32[12,192,768]{2,1,0:T(8,128)S(1)} %get-tuple-element.36, f32[12,192]{1,0:T(8,128)S(1)} %get-tuple-element.35, ...), kind=kOutput, calls=%fused_computation.79 | convolution fusion | flops 469204992 | bytes 10644480 | tf_op jit(solution)/shard_map/hqk,khe->qhe/dot_general | solution.py:54
  258.3 3.1 broadcast_in_dim.251
  261.3 6.2 %copy.237 = f32[768,12,128]{0,2,1:T(8,128)} copy(f32[768,12,128]{2,0,1:T(8,128)} %bitcast.219) | data formatting | bytes 9437184 | tf_op jit(solution)/shard_map/jit(_where)/broadcast_in_dim | solution.py:35
  268.7 6.4 %fusion.28 = bf16[768,12,128]{0,2,1:T(8,128)(2,1)S(1)} fusion(f32[768,12,128]{0,2,1:T(8,128)} %copy.237, f32[768,12,128]{0,2,1:T(8,128)} %copy.234, f32[12,128,768]{2,1,0:T(8,128)} %fusion.3, f32[768,12]{0,1:T(8,128)S(1)} %fusion.68, f32[768,12]{0,1:T(8,128)S(1)} %get-tuple-element.30, f32[768,12]{0,1:T(8,128)S(1)} %get-tuple-element.31, ...), kind=kLoop, calls=%fused_computation.45 | loop fusion | flops 11796480 | bytes 16717824 | tf_op jit(solution)/shard_map/convert_element_type | solution.py:115
  275.7 4.8 %fusion.18 = (f32[768]{0:T(1024)S(1)}, bf16[768,1536]{1,0:T(8,128)(2,1)S(1)}) fusion(bf16[768,1536]{0,1:T(8,128)(2,1)S(1)} %bitcast.237, bf16[1536,1536]{1,0:T(8,128)(2,1)S(1)} %bitcast.258, bf16[32,24,1536]{2,1,0:T(8,128)(2,1)S(1)} %copy-done.2), kind=kOutput, calls=%fused_computation.31 | convolution fusion | flops 3630955776 | bytes 11799552 | tf_op jit(solution)/shard_map/dot_general | solution.py:116
  281.9 1.9 fusion.19
  283.8 2.8 copy.243
  286.6 2.5 bitcast_reduce_fusion
  289.1 2.7 fusion.14
  293.6 1.7 collective-permute-start.10
  295.4 1.7 collective-permute-done.13
  297.5 2.9 collective-permute-start.11
  302.3 3.1 %multiply_reduce_fusion = f32[256,768]{0,1:T(8,128)S(1)} fusion(f32[12,768,256]{2,1,0:T(8,128)S(1)} %get-tuple-element.44, f32[12,256]{1,0:T(8,128)S(1)} %add_divide_fusion, f32[12,256]{1,0:T(8,128)S(1)} %get-tuple-element.43, pred[768]{0:T(1024)(128)(4,1)S(1)} %gt.82), kind=kLoop, calls=%fused_computation.18 | loop fusion | flops 13959168 | bytes 10248960 | tf_op jit(solution)/shard_map/reduce_sum | solution.py:138
  (150 shorter events, 30.1 us)
Async XLA Ops:
  6.9 14.4 %all-to-all-start.1 = ((s32[32,24,1]{1,2,0:T(1,128)}), s32[32,24,1]{1,2,0:T(1,128)S(1)}, u32[]{:S(2)}, u32[]{:S(2)}) async-start(s32[32,24,1]{1,2,0:T(1,128)} %bitcast.3), calls=%async_computation.1 | async-start | bytes 32768 | tf_op jit(solution)/shard_map/all_to_all | solution.py:84
  21.3 60.3 %copy-start.12 = (f32[1536]{0:T(1024)S(1)}, f32[1536]{0:T(1024)}, u32[]{:S(2)}) copy-start(f32[1536]{0:T(1024)} %param.8) | copy-start | bytes 18436
  21.3 59.7 %all-to-all-start = ((bf16[32,24,1536]{2,1,0:T(8,128)(2,1)}), bf16[32,24,1536]{2,1,0:T(8,128)(2,1)S(1)}, u32[]{:S(2)}, u32[]{:S(2)}) async-start(bf16[32,24,1536]{2,1,0:T(8,128)(2,1)} %bitcast.227), calls=%async_computation | async-start | bytes 4718592 | tf_op jit(solution)/shard_map/all_to_all | solution.py:83
  25.2 1.4 copy-start.13
  25.5 56.7 %copy-start.15 = (pred[2,12]{1,0:T(4,128)(4,1)}, pred[2,12]{1,0:T(4,128)(4,1)S(1)}, u32[]{:S(2)}) copy-start(pred[2,12]{1,0:T(4,128)(4,1)S(1)} %iota_compare_fusion.3) | copy-start | bytes 76
  28.2 1.3 collective-permute-start.2
  28.9 2.7 collective-permute-start
  29.7 34.5 %collective-permute-start.3 = (bf16[384,4]{0,1:T(4,128)(2,1)S(1)}, bf16[384,4]{0,1:T(4,128)(2,1)S(1)}, u32[]{:S(2)}, u32[]{:S(2)}) collective-permute-start(bf16[384,4]{0,1:T(4,128)(2,1)S(1)} %pad_maximum_fusion.8), channel_id=1, source_target_pairs={{0,2},{1,3},{2,0},{3,1},{4,6},{5,7},{6,4},{7,5},{8,10},{9,11},{10,... | collective-permute-start | bytes 9224 | tf_op jit(solution)/shard_map/ppermute | solution.py:16
  81.0 17.4 %copy-start.1 = (bf16[32,24,1536]{2,1,0:T(8,128)(2,1)}, bf16[32,24,1536]{2,1,0:T(8,128)(2,1)S(1)}, u32[]{:S(2)}) copy-start(bf16[32,24,1536]{2,1,0:T(8,128)(2,1)S(1)} %all-to-all-done) | copy-start | bytes 7077892
  108.7 6.8 %copy-start = (bf16[768,4608]{0,1:T(8,128)(2,1)S(1)}, bf16[768,4608]{0,1:T(8,128)(2,1)}, u32[]{:S(2)}) copy-start(bf16[768,4608]{0,1:T(8,128)(2,1)} %copy.200) | copy-start | bytes 21233668
  161.5 31.9 %collective-permute-start.7 = (bf16[192,12,128]{2,0,1:T(8,128)(2,1)}, bf16[192,12,128]{2,0,1:T(8,128)(2,1)}, u32[]{:S(2)}, u32[]{:S(2)}) collective-permute-start(bf16[192,12,128]{2,0,1:T(8,128)(2,1)} %bitcast.54), channel_id=1, source_target_pairs={{0,1},{1,0},{2,3},{3,2},{4,5},{5,4},{6,7},{7,6},{8,9},{9,8},{10,11... | collective-permute-start | bytes 1769480 | tf_op jit(solution)/shard_map/ppermute | solution.py:16
  173.7 4.5 %copy-start.3 = (bf16[768,1,12,128]{3,0,2,1:T(8,128)(2,1)S(1)}, bf16[768,1,12,128]{3,0,2,1:T(8,128)(2,1)}, u32[]{:S(2)}) copy-start(bf16[768,1,12,128]{3,0,2,1:T(8,128)(2,1)} %copy.257) | copy-start | bytes 7077892
  173.7 6.8 %copy-start.4 = (bf16[768,1,12,128]{3,0,2,1:T(8,128)(2,1)S(1)}, bf16[768,1,12,128]{3,0,2,1:T(8,128)(2,1)}, u32[]{:S(2)}) copy-start(bf16[768,1,12,128]{3,0,2,1:T(8,128)(2,1)} %copy.258) | copy-start | bytes 7077892
  177.8 18.0 %collective-permute-start.4 = (bf16[192,12,128]{2,0,1:T(8,128)(2,1)}, bf16[192,12,128]{2,0,1:T(8,128)(2,1)}, u32[]{:S(2)}, u32[]{:S(2)}) collective-permute-start(bf16[192,12,128]{2,0,1:T(8,128)(2,1)} %bitcast.36), channel_id=1, source_target_pairs={{0,1},{1,0},{2,3},{3,2},{4,5},{5,4},{6,7},{7,6},{8,9},{9,8},{10,11... | collective-permute-start | bytes 1769480 | tf_op jit(solution)/shard_map/ppermute | solution.py:16
  184.0 2.4 copy-start.6
  184.0 16.1 %collective-permute-start.1 = (bf16[384,12,128]{2,0,1:T(8,128)(2,1)}, bf16[384,12,128]{2,0,1:T(8,128)(2,1)}, u32[]{:S(2)}, u32[]{:S(2)}) collective-permute-start(bf16[384,12,128]{2,0,1:T(8,128)(2,1)} %bitcast.19), channel_id=1, source_target_pairs={{0,1},{1,0},{2,3},{3,2},{4,5},{5,4},{6,7},{7,6},{8,9},{9,8},{10,11... | collective-permute-start | bytes 3538952 | tf_op jit(solution)/shard_map/ppermute | solution.py:16
  188.9 19.3 %collective-permute-start.6 = (bf16[384,12,128]{0,2,1:T(8,128)(2,1)}, bf16[384,12,128]{0,2,1:T(8,128)(2,1)S(1)}, u32[]{:S(2)}, u32[]{:S(2)}) collective-permute-start(bf16[384,12,128]{0,2,1:T(8,128)(2,1)} %bitcast.240), channel_id=1, source_target_pairs={{0,1},{1,0},{2,3},{3,2},{4,5},{5,4},{6,7},{7,6},{8,9},{9,8},{10,11... | collective-permute-start | bytes 3538952 | tf_op jit(solution)/shard_map/ppermute | solution.py:16
  189.4 10.7 %copy-start.10 = (pred[768,12]{0,1:T(8,128)(4,1)S(1)}, pred[768,12]{0,1:T(8,128)(4,1)}, u32[]{:S(2)}) copy-start(pred[768,12]{0,1:T(8,128)(4,1)} %gt.72) | copy-start | bytes 27652
  195.7 58.6 %collective-permute-start.8 = (bf16[384,12,128]{2,0,1:T(8,128)(2,1)}, bf16[384,12,128]{2,0,1:T(8,128)(2,1)}, u32[]{:S(2)}, u32[]{:S(2)}) collective-permute-start(bf16[384,12,128]{2,0,1:T(8,128)(2,1)} %pad_maximum_fusion.4), channel_id=1, source_target_pairs={{0,2},{1,3},{2,0},{3,1},{4,6},{5,7},{6,4},{7,5},{8,10},{9,11},{10,... | collective-permute-start | bytes 3538952 | tf_op jit(solution)/shard_map/ppermute | solution.py:16
  198.1 51.1 %collective-permute-start.5 = (bf16[384,12,128]{2,0,1:T(8,128)(2,1)}, bf16[384,12,128]{2,0,1:T(8,128)(2,1)}, u32[]{:S(2)}, u32[]{:S(2)}) collective-permute-start(bf16[384,12,128]{2,0,1:T(8,128)(2,1)} %pad_maximum_fusion.2), channel_id=1, source_target_pairs={{0,2},{1,3},{2,0},{3,1},{4,6},{5,7},{6,4},{7,5},{8,10},{9,11},{10,... | collective-permute-start | bytes 3538952 | tf_op jit(solution)/shard_map/ppermute | solution.py:16
  203.9 4.3 %copy-start.7 = (bf16[384,6,2,1,128]{0,4,2,1,3:T(8,128)(2,1)S(1)}, bf16[384,6,2,1,128]{0,4,2,1,3:T(8,128)(2,1)}, u32[]{:S(2)}) copy-start(bf16[384,6,2,1,128]{0,4,2,1,3:T(8,128)(2,1)} %copy.232) | copy-start | bytes 3538948
  219.1 6.3 %copy-start.16 = (pred[2,12]{1,0:T(4,128)(4,1)S(1)}, pred[2,12]{1,0:T(4,128)(4,1)}, u32[]{:S(2)}) copy-start(pred[2,12]{1,0:T(4,128)(4,1)} %copy-done.15) | copy-start | bytes 76
  219.1 30.1 %copy-start.8 = (bf16[192,3,4,1,128]{4,0,3,2,1:T(8,128)(2,1)S(1)}, bf16[192,3,4,1,128]{4,0,3,2,1:T(8,128)(2,1)}, u32[]{:S(2)}) copy-start(bf16[192,3,4,1,128]{4,0,3,2,1:T(8,128)(2,1)} %pad_maximum_fusion.5) | copy-start | bytes 1769476
  219.1 30.1 %copy-start.11 = (pred[768,12]{0,1:T(8,128)(4,1)S(1)}, pred[768,12]{0,1:T(8,128)(4,1)}, u32[]{:S(2)}) copy-start(pred[768,12]{0,1:T(8,128)(4,1)} %gt.77) | copy-start | bytes 27652
  261.3 6.3 %copy-start.14 = (pred[4,12]{1,0:T(4,128)(4,1)S(1)}, pred[4,12]{1,0:T(4,128)(4,1)}, u32[]{:S(2)}) copy-start(pred[4,12]{1,0:T(4,128)(4,1)} %copy-done.13) | copy-start | bytes 148
  261.3 6.8 %copy-start.9 = (pred[768,12]{0,1:T(8,128)(4,1)S(1)}, pred[768,12]{0,1:T(8,128)(4,1)}, u32[]{:S(2)}) copy-start(pred[768,12]{0,1:T(8,128)(4,1)} %copy.225) | copy-start | bytes 27652
  261.3 13.8 %slice-start = ((s8[4718592]{0:T(1024)(128)(4,1)}), s8[524288]{0:T(1024)(128)(4,1)S(1)}, s32[]{:S(2)}) async-start(s8[4718592]{0:T(1024)(128)(4,1)} %bitcast.257), calls=%async_computation.2 | async-start | bytes 1048576
  268.7 6.4 %copy-start.2 = (bf16[32,24,1536]{2,1,0:T(8,128)(2,1)S(1)}, bf16[32,24,1536]{2,1,0:T(8,128)(2,1)}, u32[]{:S(2)}) copy-start(bf16[32,24,1536]{2,1,0:T(8,128)(2,1)} %copy-done.1) | copy-start | bytes 7077892
  268.7 7.0 %slice-start.1 = ((s8[4718592]{0:T(1024)(128)(4,1)}), s8[4194304]{0:T(1024)(128)(4,1)S(1)}, s32[]{:S(2)}) async-start(s8[4718592]{0:T(1024)(128)(4,1)} %bitcast.257), calls=%async_computation.3 | async-start | bytes 8388608
  280.5 1.4 copy-start.5
  291.9 1.2 collective-permute-start.12
  291.9 1.3 collective-permute-start.9
  293.3 3.8 %collective-permute-start.13 = (f32[12,256]{1,0:T(8,128)S(1)}, f32[12,256]{1,0:T(8,128)S(1)}, u32[]{:S(2)}, u32[]{:S(2)}) collective-permute-start(f32[12,256]{1,0:T(8,128)S(1)} %get-tuple-element.6), channel_id=1, source_target_pairs={{0,2},{1,3},{2,0},{3,1},{4,6},{5,7},{6,4},{7,5},{8,10},{9,11},{10,... | collective-permute-start | bytes 36872 | tf_op jit(solution)/shard_map/ppermute | solution.py:16
  293.6 3.7 %collective-permute-start.10 = (f32[12,256]{1,0:T(8,128)S(1)}, f32[12,256]{1,0:T(8,128)S(1)}, u32[]{:S(2)}, u32[]{:S(2)}) collective-permute-start(f32[12,256]{1,0:T(8,128)S(1)} %get-tuple-element.7), channel_id=1, source_target_pairs={{0,2},{1,3},{2,0},{3,1},{4,6},{5,7},{6,4},{7,5},{8,10},{9,11},{10,... | collective-permute-start | bytes 36872 | tf_op jit(solution)/shard_map/ppermute | solution.py:16
  297.4 4.7 %collective-permute-start.14 = (f32[12,256]{1,0:T(8,128)S(1)}, f32[12,256]{1,0:T(8,128)S(1)}, u32[]{:S(2)}, u32[]{:S(2)}) collective-permute-start(f32[12,256]{1,0:T(8,128)S(1)} %get-tuple-element.4), channel_id=1, source_target_pairs={{0,4},{1,5},{2,6},{3,7},{4,0},{5,1},{6,2},{7,3},{8,12},{9,13},{10,... | collective-permute-start | bytes 36872 | tf_op jit(solution)/shard_map/ppermute | solution.py:16
  297.5 4.7 %collective-permute-start.11 = (f32[12,256]{1,0:T(8,128)S(1)}, f32[12,256]{1,0:T(8,128)S(1)}, u32[]{:S(2)}, u32[]{:S(2)}) collective-permute-start(f32[12,256]{1,0:T(8,128)S(1)} %get-tuple-element.5), channel_id=1, source_target_pairs={{0,4},{1,5},{2,6},{3,7},{4,0},{5,1},{6,2},{7,3},{8,12},{9,13},{10,... | collective-permute-start | bytes 36872 | tf_op jit(solution)/shard_map/ppermute | solution.py:16
where the time goes:
time: 312 us; the launch traced here: 307 us
  local copies, waits for them, and re-layouts  89 us (29%)
  waiting for transfers between devices  77.9 us (25%)
  matrix products  66.4 us (21%)
  other arithmetic  49.2 us (16%)
  starting transfers between devices  22.4 us (7%)
    ppermute x15, waiting for transfers between devices, partner_2(): return lax.ppermute(value, axis, pairs)  59.5 us
    dot_general x3, matrix products, attend(): jnp.einsum('hqk,khe->qhe', exp_scores.astype(jnp.bfloat16), value, prefer...  24.1 us
    broadcast_in_dim x13, local copies, waits for them, and re-layouts, spread_back(): widened = jnp.where(chosen, rows[:, None], jnp.asarray(fill, rows.dtype))  21 us
    reduce_sum x3, other arithmetic, attend(): total = jnp.sum(exp_scores, axis=2)  19.8 us
    dot_general x3, matrix products, attend(): jnp.einsum('qhe,khe->hqk', query, key_rows, preferred_element_type=jnp.fl...  18.9 us
    dot_general x1, matrix products, shards(): jnp.dot(normed, qkv_weight, preferred_element_type=jnp.float32)  16.1 us
    all_to_all x1, waiting for transfers between devices, shards(): lax.all_to_all(buffer, ('slide', 'seq'), split_axis=0, concat_axis=0, til...  16.1 us
    unnamed x52, local copies, waits for them, and re-layouts  14.7 us
  transfers between devices with their start and end apart: 17, of which 10 were waited for; matrix products, arithmetic and copies ran while one was open for 25% of the time, Pallas kernels for 0%

commit v1 on v0

v1 whole, which is shorter than its diff:
```python
import functools
import math

import jax
import jax.numpy as jnp
from jax import lax
from jax.experimental import pallas as pl
from jax.experimental.pallas import tpu as pltpu
from jax.sharding import PartitionSpec as P

HEADS = 12
HEAD = 128
GROUP = 4
WIDE = GROUP * HEAD
MASKED = -1e30
EPSILON = 1e-06
FACTOR = math.log2(math.e) / math.sqrt(HEAD)
F32 = jnp.float32
BF16 = jnp.bfloat16
QUARTER_OF = (0, 2, 1, 3)
VMEM_LIMIT = 56 * 1024 * 1024


def params(**more):
    return pltpu.CompilerParams(vmem_limit_bytes=VMEM_LIMIT, **more)


def dispatch_kernel(capacity, col_ref, row_ref, embeds_ref, buffer_ref, counts_ref):
    rows = embeds_ref.shape[0]
    slots = buffer_ref.shape[0]
    col = col_ref[...]
    row = row_ref[...]
    first = lax.broadcasted_iota(jnp.int32, (rows, rows), 0)
    second = lax.broadcasted_iota(jnp.int32, (rows, rows), 1)
    same = jnp.logical_and(col == row, first < second)
    rank = jnp.sum(same.astype(F32), axis=0, keepdims=True).astype(jnp.int32)
    place = row * capacity + rank
    lanes = lax.broadcasted_iota(jnp.int32, (rows, counts_ref.shape[1]), 1)
    counts_ref[...] = jnp.sum((col == lanes).astype(F32), axis=0, keepdims=True).astype(jnp.int32)
    chosen = (lax.broadcasted_iota(jnp.int32, (slots, rows), 0) == place).astype(F32).astype(BF16)
    for start in range(0, embeds_ref.shape[1], WIDE):
        part = embeds_ref[:, start : start + WIDE]
        buffer_ref[:, start : start + WIDE] = jnp.dot(
            chosen, part, preferred_element_type=F32
        ).astype(BF16)


def dispatch(destination, embeds, devices, capacity):
    rows, width = embeds.shape
    slots = devices * capacity
    return pl.pallas_call(
        functools.partial(dispatch_kernel, capacity),
        out_shape=(
            jax.ShapeDtypeStruct((slots, width), BF16),
            jax.ShapeDtypeStruct((1, max(128, devices)), jnp.int32),
        ),
        compiler_params=params(),
        name="dispatch",
    )(destination, destination.reshape(1, rows), embeds)


def original_of(index, quarter):
    block = (
        (index >= quarter).astype(jnp.int32)
        + (index >= 2 * quarter).astype(jnp.int32)
        + (index >= 3 * quarter).astype(jnp.int32)
    )
    phase = 2 * jnp.where((block == 1) | (block == 3), 1, 0) + (block >= 2).astype(jnp.int32)
    return 4 * (index - quarter * block) + phase


def project_kernel(tiles_ref, gain_ref, weight_ref, out_ref, near_ref, far_ref, normed_ref):
    step = pl.program_id(0)
    slots, width = tiles_ref.shape
    quarter = slots // 4
    half = slots // 2

    @pl.when(step == 0)
    def _():
        tile = tiles_ref[...].astype(F32)
        mean = jnp.mean(tile * tile, axis=1, keepdims=True)
        normed = (tile * lax.rsqrt(mean + EPSILON) * gain_ref[...]).astype(BF16)
        index = lax.broadcasted_iota(jnp.int32, (slots, slots), 0)
        position = lax.broadcasted_iota(jnp.int32, (slots, slots), 1)
        order = (original_of(index, quarter) == position).astype(F32).astype(BF16)
        for start in range(0, width, WIDE):
            normed_ref[:, start : start + WIDE] = jnp.dot(
                order, normed[:, start : start + WIDE], preferred_element_type=F32
            ).astype(BF16)

    value = jnp.dot(normed_ref[...], weight_ref[...], preferred_element_type=F32).astype(BF16)
    out_ref[...] = value

    @pl.when(step >= 3)
    def _():
        for j in range(GROUP):
            cols = slice(j * HEAD, (j + 1) * HEAD)
            near_ref[:, cols] = value[(j % 2) * half : (j % 2 + 1) * half, cols]
            begin = QUARTER_OF[j] * quarter
            far_ref[:, cols] = value[begin : begin + quarter, cols]


def project(tiles, gain, weight):
    slots, width = tiles.shape
    steps = weight.shape[1] // WIDE
    tail = lambda i: (0, jnp.maximum(i - steps // 3, 0))
    return pl.pallas_call(
        project_kernel,
        grid=(steps,),
        in_specs=[
            pl.BlockSpec((slots, width), lambda i: (0, 0)),
            pl.BlockSpec((1, width), lambda i: (0, 0)),
            pl.BlockSpec((width, WIDE), lambda i: (0, i)),
        ],
        out_specs=[
            pl.BlockSpec((slots, WIDE), lambda i: (0, i)),
            pl.BlockSpec((slots // 2, WIDE), tail),
            pl.BlockSpec((slots // 4, WIDE), tail),
        ],
        out_shape=(
            jax.ShapeDtypeStruct((slots, 3 * width), BF16),
            jax.ShapeDtypeStruct((slots // 2, 2 * width), BF16),
            jax.ShapeDtypeStruct((slots // 4, 2 * width), BF16),
        ),
        scratch_shapes=[pltpu.VMEM((slots, width), BF16)],
        compiler_params=params(),
        cost_estimate=pl.CostEstimate(
            flops=2 * slots * width * 3 * width, bytes_accessed=30_000_000, transcendentals=0
        ),
        name="project",
    )(tiles, gain.reshape(1, width), weight)


def softmax_parts(query, keys, values, bias):
    scores = lax.dot_general(
        query, keys, (((1,), (1,)), ((), ())), preferred_element_type=F32
    )
    scores = scores * FACTOR + bias
    peak = jnp.max(scores, axis=1, keepdims=True)
    weights = jnp.exp2(scores - peak)
    total = jnp.sum(weights, axis=1, keepdims=True)
    summed = jnp.dot(weights.astype(BF16), values, preferred_element_type=F32)
    return summed, peak, total


def near_attention_kernel(q_ref, k_ref, v_ref, bias_ref, summed_ref, stats_ref):
    slots = q_ref.shape[0]
    half = slots // 2
    lanes = lax.broadcasted_iota(jnp.int32, (half, HEAD), 1)
    bias = bias_ref[0:1, :]
    for part in range(2):
        rows = slice(part * half, (part + 1) * half)
        stats = jnp.zeros((half, HEAD), F32)
        for j in range(GROUP):
            cols = slice(j * HEAD, (j + 1) * HEAD)
            summed, peak, total = softmax_parts(q_ref[rows, cols], k_ref[:, cols], v_ref[:, cols], bias)
            summed_ref[rows, cols] = summed
            stats = jnp.where(lanes == 2 * j, peak, jnp.where(lanes == 2 * j + 1, total, stats))
        stats_ref[rows, :] = stats


def near_attention(projected, bias):
    slots, triple = projected.shape
    width = triple // 3
    steps = width // WIDE
    return pl.pallas_call(
        near_attention_kernel,
        grid=(steps,),
        in_specs=[
            pl.BlockSpec((slots, WIDE), lambda i: (0, i)),
            pl.BlockSpec((slots, WIDE), lambda i: (0, i + steps)),
            pl.BlockSpec((slots, WIDE), lambda i: (0, i + 2 * steps)),
            pl.BlockSpec(bias.shape, lambda i: (0, 0)),
        ],
        out_specs=[
            pl.BlockSpec((slots, WIDE), lambda i: (0, i)),
            pl.BlockSpec((slots, HEAD), lambda i: (0, i)),
        ],
        out_shape=(
            jax.ShapeDtypeStruct((slots, width), F32),
            jax.ShapeDtypeStruct((slots, steps * HEAD), F32),
        ),
        compiler_params=params(),
        cost_estimate=pl.CostEstimate(
            flops=8 * slots * slots * width,
            bytes_accessed=14_000_000,
            transcendentals=4 * slots * slots * HEADS,
        ),
        name="near_attention",
    )(projected, projected, projected, bias)


def combine(parts):
    top = parts[0][1]
    for _, peak, _ in parts[1:]:
        top = jnp.maximum(top, peak)
    above, below = 0.0, 0.0
    for summed, peak, total in parts:
        factor = jnp.exp2(peak - top)
        above = above + factor * summed
        below = below + factor * total
    return (above * (1.0 / jnp.maximum(below, 1.0))).astype(BF16)


def far_attention_kernel(
    q_ref, k_ref, v_ref, bias_ref, pair_k, pair_v, one_k, one_v, two_k, two_v,
    summed_ref, stats_ref, mixed_ref,
):
    slots = q_ref.shape[0]
    half, quarter = slots // 2, slots // 4
    for j in range(GROUP):
        cols = slice(j * HEAD, (j + 1) * HEAD)
        start = (j % 2) * half
        begin = QUARTER_OF[j] * quarter
        inside = begin - start
        mine = slice(start, start + half)
        fourth = slice(begin, begin + quarter)
        within = slice(inside, inside + quarter)

        def local(rows):
            return (
                summed_ref[rows, cols],
                stats_ref[rows, 2 * j : 2 * j + 1],
                stats_ref[rows, 2 * j + 1 : 2 * j + 2],
            )

        keys = jnp.concatenate([k_ref[mine, cols], pair_k[:, cols]], axis=0)
        values = jnp.concatenate([v_ref[mine, cols], pair_v[:, cols]], axis=0)
        two = softmax_parts(q_ref[mine, cols], keys, values, bias_ref[1 + j % 2 : 2 + j % 2, :])
        keys = jnp.concatenate(
            [k_ref[fourth, cols], pair_k[within, cols], one_k[:, cols], two_k[:, cols]], axis=0
        )
        values = jnp.concatenate(
            [v_ref[fourth, cols], pair_v[within, cols], one_v[:, cols], two_v[:, cols]], axis=0
        )
        four = softmax_parts(q_ref[fourth, cols], keys, values, bias_ref[3 + j : 4 + j, :])
        other = slice(half - start, 2 * half - start)
        mixed_ref[other, cols] = combine([local(other)])
        for offset in (0, quarter):
            rows = slice(start + offset, start + offset + quarter)
            parts = [local(rows), tuple(x[offset : offset + quarter] for x in two)]
            if offset == inside:
                parts.append(four)
            mixed_ref[rows, cols] = combine(parts)


def far_attention(projected, bias, pair, one, two, summed, stats):
    slots, triple = projected.shape
    width = triple // 3
    steps = width // WIDE

    def twice(array):
        rows = array.shape[0]
        return [
            pl.BlockSpec((rows, WIDE), lambda i: (0, i)),
            pl.BlockSpec((rows, WIDE), lambda i: (0, i + steps)),
        ]

    return pl.pallas_call(
        far_attention_kernel,
        grid=(steps,),
        in_specs=[
            pl.BlockSpec((slots, WIDE), lambda i: (0, i)),
            pl.BlockSpec((slots, WIDE), lambda i: (0, i + steps)),
            pl.BlockSpec((slots, WIDE), lambda i: (0, i + 2 * steps)),
            pl.BlockSpec(bias.shape, lambda i: (0, 0)),
            *twice(pair),
            *twice(one),
            *twice(two),
            pl.BlockSpec((slots, WIDE), lambda i: (0, i)),
            pl.BlockSpec((slots, HEAD), lambda i: (0, i)),
        ],
        out_specs=pl.BlockSpec((slots, WIDE), lambda i: (0, i)),
        out_shape=jax.ShapeDtypeStruct((slots, width), BF16),
        compiler_params=params(),
        name="far_attention",
    )(projected, projected, projected, bias, pair, pair, one, one, two, two, summed, stats)


def finish_kernel(mixed_ref, tiles_ref, weight_ref, finding_ref, mask_ref, layer_ref, keys_ref, stats_ref, plain_ref):
    slots, width = tiles_ref.shape
    quarter = slots // 4
    position = lax.broadcasted_iota(jnp.int32, (slots, slots), 0)
    index = lax.broadcasted_iota(jnp.int32, (slots, slots), 1)
    order = (original_of(index, quarter) == position).astype(F32).astype(BF16)
    for start in range(0, width, WIDE):
        plain_ref[:, start : start + WIDE] = jnp.dot(
            order, mixed_ref[:, start : start + WIDE], preferred_element_type=F32
        ).astype(BF16)
    square = jnp.zeros((slots, 1), F32)
    for start in range(0, width, WIDE):
        cols = slice(start, start + WIDE)
        added = jnp.dot(plain_ref[...], weight_ref[:, cols], preferred_element_type=F32)
        out = (tiles_ref[:, cols].astype(F32) + added).astype(BF16)
        layer_ref[:, cols] = out
        wide = out.astype(F32)
        square = square + jnp.sum(wide * wide, axis=1, keepdims=True)
    inverse = lax.rsqrt(square * (1.0 / width) + EPSILON)
    mask = mask_ref[...]
    for h in range(HEADS):
        cols = slice(h * HEAD, (h + 1) * HEAD)
        keys = (layer_ref[:, cols].astype(F32) * inverse).astype(BF16)
        keys_ref[:, cols] = keys
        scores = lax.dot_general(
            keys, finding_ref[:, cols], (((1,), (1,)), ((), ())), preferred_element_type=F32
        )
        scores = scores * FACTOR + mask
        peak = jnp.max(scores, axis=0, keepdims=True)
        stats_ref[h : h + 1, :] = peak
        stats_ref[HEADS + h : HEADS + h + 1, :] = jnp.sum(
            jnp.exp2(scores - peak), axis=0, keepdims=True
        )


def finish(mixed, tiles, weight, finding, mask):
    slots, width = tiles.shape
    return pl.pallas_call(
        finish_kernel,
        out_shape=(
            jax.ShapeDtypeStruct((slots, width), BF16),
            jax.ShapeDtypeStruct((slots, width), BF16),
            jax.ShapeDtypeStruct((2 * HEADS, finding.shape[0]), F32),
        ),
        scratch_shapes=[pltpu.VMEM((slots, width), BF16)],
        compiler_params=params(),
        name="finish",
    )(mixed, tiles, weight, finding, mask)


def heat_kernel(count, scale, stats_ref, keys_ref, finding_ref, mask_ref, heat_ref, held, send_sem, recv_sem):
    slide = lax.axis_index("slide")
    me = lax.axis_index("seq")
    barrier = pltpu.get_barrier_semaphore()
    for hop in range(1, count):
        peer = lax.rem(me + hop, count)
        pl.semaphore_signal(
            barrier, inc=1, device_id=(slide, peer), device_id_type=pl.DeviceIdType.MESH
        )
    pl.semaphore_wait(barrier, count - 1)
    copies = []
    for hop in range(1, count):
        peer = lax.rem(me + hop, count)
        copy = pltpu.make_async_remote_copy(
            src_ref=stats_ref,
            dst_ref=held.at[hop],
            send_sem=send_sem.at[hop],
            recv_sem=recv_sem.at[hop],
            device_id=(slide, peer),
            device_id_type=pl.DeviceIdType.MESH,
        )
        copy.start()
        copies.append(copy)
    for copy in copies:
        copy.wait()
    everything = [stats_ref[...]] + [held[hop] for hop in range(1, count)]
    peaks = everything[0][:HEADS]
    for part in everything[1:]:
        peaks = jnp.maximum(peaks, part[:HEADS])
    totals = jnp.zeros_like(peaks)
    for part in everything:
        totals = totals + part[HEADS:] * jnp.exp2(part[:HEADS] - peaks)
    factors = scale / totals
    slots = keys_ref.shape[0]
    chunk = slots // 2
    for start in range(0, slots, chunk):
        rows = slice(start, start + chunk)
        mask = mask_ref[rows, :]
        total = jnp.zeros((chunk, finding_ref.shape[0]), F32)
        for h in range(HEADS):
            cols = slice(h * HEAD, (h + 1) * HEAD)
            scores = lax.dot_general(
                keys_ref[rows, cols], finding_ref[:, cols], (((1,), (1,)), ((), ())),
                preferred_element_type=F32,
            )
            scores = scores * FACTOR + mask
            total = total + jnp.exp2(scores - peaks[h : h + 1]) * factors[h : h + 1]
        heat_ref[rows, :] = total


def heat_map(count, stats, keys, finding, mask):
    slots = keys.shape[0]
    finds = finding.shape[0]
    return pl.pallas_call(
        functools.partial(heat_kernel, count, count * slots / HEADS),
        in_specs=[pl.BlockSpec(memory_space=pltpu.VMEM)] * 4,
        out_specs=pl.BlockSpec(memory_space=pltpu.VMEM),
        out_shape=jax.ShapeDtypeStruct((slots, finds), F32),
        scratch_shapes=[
            pltpu.VMEM((count, 2 * HEADS, finds), F32),
            pltpu.SemaphoreType.DMA((count,)),
            pltpu.SemaphoreType.DMA((count,)),
        ],
        compiler_params=params(collective_id=0, has_side_effects=True),
        name="heat_map",
    )(stats, keys, finding, mask)


def exchange(value, mask):
    pairs = [(source, source ^ mask) for source in range(lax.axis_size("seq"))]
    return lax.ppermute(value, "seq", pairs)


def shards(embeds, destination, norm_gain, qkv_weight, out_weight, finding_queries):
    devices = lax.axis_size(("slide", "seq"))
    seq_count = lax.axis_size("seq")
    slots = embeds.shape[0] * 2
    capacity = slots // devices
    half, quarter = slots // 2, slots // 4
    buffer, counts = dispatch(destination, embeds, devices, capacity)
    counts = lax.all_gather(counts[0], ("slide", "seq"))[:, :devices]
    tiles = lax.all_to_all(buffer, ("slide", "seq"), split_axis=0, concat_axis=0, tiled=True)

    me = lax.axis_index(("slide", "seq"))
    wanted = (me ^ jnp.arange(4, dtype=jnp.int32))[:, None] == jnp.arange(devices, dtype=jnp.int32)
    reached = jnp.sum(jnp.where(wanted[:, None, :], counts[None], 0), axis=2)
    open_slots = jnp.arange(capacity, dtype=jnp.int32)[None, None, :] < reached[:, :, None]
    bias = jnp.where(open_slots, 0.0, MASKED).astype(F32).reshape(4, slots)
    mask = bias[0].reshape(slots, 1)
    phased = bias.reshape(4, quarter, 4).transpose(0, 2, 1)
    phased = jnp.stack([phased[:, 0], phased[:, 2], phased[:, 1], phased[:, 3]], axis=1)
    rows = [phased[0].reshape(slots)]
    for parity in range(2):
        rows.append(phased[:2, 2 * parity : 2 * parity + 2].reshape(slots))
    for phase in range(4):
        rows.append(phased[:, QUARTER_OF[phase]].reshape(slots))
    rows.append(rows[0])
    bias = jnp.stack(rows)

    projected, near, far = project(tiles, norm_gain, qkv_weight)
    one = exchange(far, 2)
    pair = exchange(near, 1)
    summed, stats = near_attention(projected, bias)
    two = exchange(one, 1)
    mixed = far_attention(projected, bias, pair, one, two, summed, stats)
    layer_out, keys, stats = finish(mixed, tiles, out_weight, finding_queries, mask)
    heat = heat_map(seq_count, stats, keys, finding_queries, mask)
    return (layer_out, heat)


def solution(mesh):
    in_specs = (P(("slide", "seq"), None), P(("slide", "seq"), None), P(), P(), P(), P())
    out_specs = (P(("slide", "seq"), None), P(("slide", "seq"), None))
    return jax.shard_map(shards, mesh=mesh, in_specs=in_specs, out_specs=out_specs, check_vma=False)
```

time: 312 us -> 240 us (0.77)
  Pallas kernels: 0 us -> 87.4 us
  matrix products: 66.4 us -> 0 us
  local copies, waits for them, and re-layouts: 89 us -> 24.5 us
  blocking collectives: 0 us -> 59.9 us
  other arithmetic: 49.2 us -> 2.14 us
  waiting for transfers between devices: 77.9 us -> 55.2 us
  starting transfers between devices: 22.4 us -> 7.72 us
    pallas_call x0 -> x6, Pallas kernels: none -> 87.4 us  [the longest x1 24.8 us: far_attention(): pl.pallas_call(far_attention_kernel, grid=(steps,), in_specs=[pl.BlockSpe...]
    dot_general x9 -> x0, matrix products: 66.4 us -> none  [the longest x3 24.1 us: attend(): jnp.einsum('hqk,khe->qhe', exp_scores.astype(jnp.bfloat16), value, prefer...]
    all_gather x0 -> x1, blocking collectives: none -> 59.9 us  [shards(): counts = lax.all_gather(counts[0], ('slide', 'seq'))[:, :devices]]
    ppermute x15 -> x3, waiting for transfers between devices: 59.5 us -> 0.01 us  [exchange(): return lax.ppermute(value, 'seq', pairs)]
    all_to_all x1, waiting for transfers between devices: 16.1 us -> 55.2 us  [shards(): lax.all_to_all(buffer, ('slide', 'seq'), split_axis=0, concat_axis=0, til...]
    reduce_sum x8 -> x1, other arithmetic: 26.5 us -> 0.15 us  [shards(): reached = jnp.sum(jnp.where(wanted[:, None, :], counts[None], 0), axis=2)]
    slice x9 -> x2, local copies, waits for them, and re-layouts: 24.2 us -> 1.87 us  [the longest x1 1.22 us: shards(): mask = bias[0].reshape(slots, 1)]
    broadcast_in_dim x13 -> x0, local copies, waits for them, and re-layouts: 21 us -> none  [spread_back(): widened = jnp.where(chosen, rows[:, None], jnp.asarray(fill, rows.dtype))]
  transfers between devices with their start and end apart: 17 -> 4, of which waited for: 10 -> 1; matrix products, arithmetic and copies ran while one was open for 25% -> 8% of each run, Pallas kernels for 0% -> 6%
where the time goes in v1:
time: 240 us; the launch traced here: 238 us
  Pallas kernels  87.4 us (36%)
  blocking collectives  59.9 us (25%)
  waiting for transfers between devices  55.2 us (23%)
  local copies, waits for them, and re-layouts  24.5 us (10%)
  starting transfers between devices  7.72 us (3%)
    all_gather x1, blocking collectives, shards(): counts = lax.all_gather(counts[0], ('slide', 'seq'))[:, :devices]  59.9 us
    all_to_all x1, waiting for transfers between devices, shards(): lax.all_to_all(buffer, ('slide', 'seq'), split_axis=0, concat_axis=0, til...  55.2 us
    pallas_call x1, Pallas kernels, far_attention(): pl.pallas_call(far_attention_kernel, grid=(steps,), in_specs=[pl.BlockSpe...  24.8 us
    pallas_call x1, Pallas kernels, project(): pl.pallas_call(project_kernel, grid=(steps,), in_specs=[pl.BlockSpec((slo...  20.3 us
    pallas_call x1, Pallas kernels, finish(): pl.pallas_call(finish_kernel, out_shape=(jax.ShapeDtypeStruct((slots, wid...  13.8 us
    pallas_call x1, Pallas kernels, near_attention(): pl.pallas_call(near_attention_kernel, grid=(steps,), in_specs=[pl.BlockSp...  13.1 us
    pallas_call x1, Pallas kernels, heat_map(): pl.pallas_call(functools.partial(heat_kernel, count, count * slots / HEAD...  11 us
    another operation x8, local copies, waits for them, and re-layouts, shards(): bias = jnp.stack(rows)  10.8 us
  transfers between devices with their start and end apart: 4, of which 1 were waited for; matrix products, arithmetic and copies ran while one was open for 8% of the time, Pallas kernels for 6%

profile of v1, /device:TPU:0, one launch (start us, length us, event | category | flops | bytes accessed | tf_op | source)
XLA Modules:
  0.0 237.5 jit_solution(2409941311035066922)
XLA Ops:
  0.6 1.5 copy.15.col_ref
  2.1 4.3 %dispatch.1 = (bf16[768,1536]{1,0:T(8,128)(2,1)}, s32[1,128]{1,0:T(1,128)}) custom-call(s32[384,1]{1,0:T(8,128)} %copy.15.col_ref, s32[1,384]{1,0:T(1,128)} %bitcast.14, bf16[384,1536]{1,0:T(8,128)(2,1)} %embeds_ref.1), custom_call_target="tpu_custom_call" | custom-call | tf_op jit(solution)/shard_map/dispatch/pallas_call | solution.py:51
  6.5 0.0 copy-start.4
  6.5 7.3 %all-to-all-start = ((bf16[32,24,1536]{2,1,0:T(8,128)(2,1)}), bf16[32,24,1536]{2,1,0:T(8,128)(2,1)S(1)}, u32[]{:S(2)}, u32[]{:S(2)}) async-start(bf16[32,24,1536]{2,1,0:T(8,128)(2,1)} %bitcast.11), calls=%async_computation | async-start | bytes 4718592 | tf_op jit(solution)/shard_map/all_to_all | solution.py:411
  13.8 0.0 copy-done.4
  13.8 0.6 reshape.43.gain_ref
  14.4 55.2 %all-to-all-done = bf16[32,24,1536]{2,1,0:T(8,128)(2,1)S(1)} async-done(((bf16[32,24,1536]{2,1,0:T(8,128)(2,1)}), bf16[32,24,1536]{2,1,0:T(8,128)(2,1)S(1)}, u32[]{:S(2)}, u32[]{:S(2)}) %all-to-all-start) | async-done | bytes 2359328 | tf_op jit(solution)/shard_map/all_to_all | solution.py:411
  69.6 0.0 copy-start.1
  69.6 1.5 copy-done.1
  71.1 20.3 %project.1 = (bf16[768,4608]{1,0:T(8,128)(2,1)}, bf16[384,3072]{1,0:T(8,128)(2,1)}, bf16[192,3072]{1,0:T(8,128)(2,1)}) custom-call(bf16[768,1536]{1,0:T(8,128)(2,1)} %bitcast.9, f32[1,1536]{1,0:T(1,128)} %reshape.43.gain_ref, bf16[1536,4608]{1,0:T(8,128)(2,1)} %weight_ref.2), custom_call_target="tpu_custom_call" | custom-call | flops 10871635968 | bytes 30000000 | tf_op jit(solution)/shard_map/project/pallas_call | solution.py:107
  91.4 0.0 collective-permute-start.1
  91.4 0.1 collective-permute-start
  91.5 0.0 copy-done.5
  91.5 59.9 %all-gather = s32[32,1,128]{2,1,0:T(1,128)S(1)} all-gather(s32[1,1,128]{2,1,0:T(1,128)S(1)} %bitcast.15), channel_id=1, replica_groups=mesh['slide'=4,'seq'=8] {'slide','seq'}, dimensions={0}, use_global_device_ids=true | all-gather | bytes 16896 | tf_op jit(solution)/shard_map/all_gather | solution.py:410
  151.3 0.1 iota_compare_fusion.1
  151.4 0.2 select_reduce_fusion
  151.6 0.6 copy-done.3
  152.2 0.7 lt.44
  152.9 0.9 lt.45
  153.8 0.6 lt.40
  154.5 0.9 lt.41
  155.4 0.0 collective-permute-done.1.one_k.one_v
  155.4 0.0 copy-start.2
  155.4 0.4 collective-permute-start.2
  155.8 0.7 slice_reduce_fusion
  156.5 1.2 slice.44
  157.7 0.6 pad_maximum_fusion.2
  158.3 1.4 stack_reshape_squeeze.4
  159.6 0.6 pad_maximum_fusion
  160.2 1.3 stack_reshape.6
  161.6 1.4 stack_reshape.7
  162.9 1.3 stack_reshape_squeeze_stack_squeeze.12
  164.3 1.4 stack_reshape_squeeze_stack_squeeze.13
  165.6 1.3 stack_reshape_squeeze_stack_squeeze.14
  167.0 1.4 stack_reshape_squeeze_stack_squeeze.15
  168.3 0.7 fusion
  169.0 0.9 reshape_squeeze.4.mask_ref
  169.9 1.4 stack.13.bias_ref
  171.4 13.1 %near_attention.1 = (f32[768,1536]{1,0:T(8,128)}, f32[768,384]{1,0:T(8,128)}) custom-call(bf16[768,4608]{1,0:T(8,128)(2,1)} %get-tuple-element.13.q_ref.k_ref.v_ref, bf16[768,4608]{1,0:T(8,128)(2,1)} %get-tuple-element.13.q_ref.k_ref.v_ref, bf16[768,4608]{1,0:T(8,128)(2,1)} %get-tuple-element.13.q_ref.k_ref.v_ref, f32[8,768]{1,0:T(8,128)} %stack.13.bias_ref), custom_call_target="tpu_custom_call" | custom-call | flops 7247757312 | bytes 14000000 | tf_op jit(solution)/shard_map/near_attention/pallas_call | solution.py:166
  184.4 0.0 copy-done.2
  184.4 0.0 collective-permute-done.pair_k.pair_v
  184.4 0.0 copy-start
  184.5 0.0 collective-permute-done.2.two_k.two_v
  184.5 1.4 copy-done
  185.8 24.8 %far_attention.1.mixed_ref = bf16[768,1536]{1,0:T(8,128)(2,1)} custom-call(bf16[768,4608]{1,0:T(8,128)(2,1)} %get-tuple-element.13.q_ref.k_ref.v_ref, bf16[768,4608]{1,0:T(8,128)(2,1)} %get-tuple-element.13.q_ref.k_ref.v_ref, bf16[768,4608]{1,0:T(8,128)(2,1)} %get-tuple-element.13.q_ref.k_ref.v_ref, f32[8,768]{1,0:T(8,128)} %stack.13.bias_ref, ...), custom_call_target="tpu_custom_call" | custom-call | tf_op jit(solution)/shard_map/far_attention/pallas_call | solution.py:259
  210.6 13.8 %finish.1 = (bf16[768,1536]{1,0:T(8,128)(2,1)}, bf16[768,1536]{1,0:T(8,128)(2,1)}, f32[24,256]{1,0:T(8,128)}) custom-call(bf16[768,1536]{1,0:T(8,128)(2,1)} %far_attention.1.mixed_ref, bf16[768,1536]{1,0:T(8,128)(2,1)} %bitcast.10, bf16[1536,1536]{1,0:T(8,128)(2,1)} %weight_ref.3, bf16[256,1536]{1,0:T(8,128)(2,1)} %finding_ref.3, ...), custom_call_target="tpu_custom_call" | custom-call | tf_op jit(solution)/shard_map/finish/pallas_call | solution.py:317
  224.4 11.0 %heat_map.1 = f32[768,256]{1,0:T(8,128)} custom-call(f32[24,256]{1,0:T(8,128)} %get-tuple-element.20.stats_ref, bf16[768,1536]{1,0:T(8,128)(2,1)} %get-tuple-element.21.keys_ref, bf16[256,1536]{1,0:T(8,128)(2,1)} %finding_ref.3, f32[768,1]{1,0:T(8,128)} %reshape_squeeze.4.mask_ref), custom_call_target="tpu_custom_call" | custom-call | tf_op jit(solution)/shard_map/heat_map/pallas_call | solution.py:383
  235.5 2.1 copy.19
  (5 shorter events, 0.0 us)
Async XLA Ops:
  6.5 7.3 %copy-start.4 = (f32[1536]{0:T(1024)S(1)}, f32[1536]{0:T(1024)}, u32[]{:S(2)}) copy-start(f32[1536]{0:T(1024)} %param.8) | copy-start | bytes 18436
  6.5 63.1 %all-to-all-start = ((bf16[32,24,1536]{2,1,0:T(8,128)(2,1)}), bf16[32,24,1536]{2,1,0:T(8,128)(2,1)S(1)}, u32[]{:S(2)}, u32[]{:S(2)}) async-start(bf16[32,24,1536]{2,1,0:T(8,128)(2,1)} %bitcast.11), calls=%async_computation | async-start | bytes 4718592 | tf_op jit(solution)/shard_map/all_to_all | solution.py:411
  69.6 1.5 copy-start.1
  71.1 20.4 %copy-start.5 = (s32[1,128]{1,0:T(1,128)S(1)}, s32[1,128]{1,0:T(1,128)}, u32[]{:S(2)}) copy-start(s32[1,128]{1,0:T(1,128)} %get-tuple-element.14) | copy-start | bytes 1540
  91.4 64.0 %collective-permute-start.1 = (bf16[192,3072]{1,0:T(8,128)(2,1)}, bf16[192,3072]{1,0:T(8,128)(2,1)S(1)}, u32[]{:S(2)}, u32[]{:S(2)}) collective-permute-start(bf16[192,3072]{1,0:T(8,128)(2,1)} %get-tuple-element.16), channel_id=1, source_target_pairs={{0,2},{1,3},{2,0},{3,1},{4,6},{5,7},{6,4},{7,5},{8,10},{9,11},{10,... | collective-permute-start | bytes 3538952 | tf_op jit(solution)/shard_map/ppermute | solution.py:400
  91.4 93.0 %collective-permute-start = (bf16[384,3072]{1,0:T(8,128)(2,1)}, bf16[384,3072]{1,0:T(8,128)(2,1)S(1)}, u32[]{:S(2)}, u32[]{:S(2)}) collective-permute-start(bf16[384,3072]{1,0:T(8,128)(2,1)} %get-tuple-element.15), channel_id=1, source_target_pairs={{0,1},{1,0},{2,3},{3,2},{4,5},{5,4},{6,7},{7,6},{8,9},{9,8},{10,11... | collective-permute-start | bytes 7077896 | tf_op jit(solution)/shard_map/ppermute | solution.py:400
  151.6 0.6 copy-start.3
  155.4 29.0 %copy-start.2 = (bf16[192,3072]{1,0:T(8,128)(2,1)}, bf16[192,3072]{1,0:T(8,128)(2,1)S(1)}, u32[]{:S(2)}) copy-start(bf16[192,3072]{1,0:T(8,128)(2,1)S(1)} %collective-permute-done.1.one_k.one_v) | copy-start | bytes 3538948
  155.4 29.0 %collective-permute-start.2 = (bf16[192,3072]{1,0:T(8,128)(2,1)S(1)}, bf16[192,3072]{1,0:T(8,128)(2,1)}, u32[]{:S(2)}, u32[]{:S(2)}) collective-permute-start(bf16[192,3072]{1,0:T(8,128)(2,1)S(1)} %collective-permute-done.1.one_k.one_v), channel_id=1, source_target_pairs={{0,1},{1,0},{2,3},{3,2},{4,5},{5,4},{6,7},{7,6},{8,9},{9,8},{10,11... | collective-permute-start | bytes 3538952 | tf_op jit(solution)/shard_map/ppermute | solution.py:400
  184.4 1.4 copy-start

commit v2 on v1

--- a/solution.py
+++ b/solution.py
@@ -69,7 +69,143 @@
     return 4 * (index - quarter * block) + phase
 
 
-def project_kernel(tiles_ref, gain_ref, weight_ref, out_ref, near_ref, far_ref, normed_ref):
+def route_kernel(devices, seq_count, buffer_ref, counts_ref, tiles_ref, all_ref, send, recv, count_send, count_recv, own_sem):
+    me = lax.axis_index("slide") * seq_count + lax.axis_index("seq")
+    barrier = pltpu.get_barrier_semaphore()
+
+    def place_of(hop):
+        peer = lax.rem(me + hop, devices)
+        return peer, (peer // seq_count, lax.rem(peer, seq_count))
+
+    def greet(hop, carry):
+        pl.semaphore_signal(
+            barrier, inc=1, device_id=place_of(hop)[1], device_id_type=pl.DeviceIdType.MESH
+        )
+        return carry
+
+    lax.fori_loop(1, devices, greet, 0)
+    pl.semaphore_wait(barrier, devices - 1)
+
+    def copies(hop):
+        peer, where = place_of(hop)
+        rows = pltpu.make_async_remote_copy(
+            src_ref=buffer_ref.at[peer],
+            dst_ref=tiles_ref.at[me],
+            send_sem=send.at[hop],
+            recv_sem=recv.at[hop],
+            device_id=where,
+            device_id_type=pl.DeviceIdType.MESH,
+        )
+        count = pltpu.make_async_remote_copy(
+            src_ref=counts_ref.at[0],
+            dst_ref=all_ref.at[me],
+            send_sem=count_send.at[hop],
+            recv_sem=count_recv.at[hop],
+            device_id=where,
+            device_id_type=pl.DeviceIdType.MESH,
+        )
+        return rows, count
+
+    def begin(hop, carry):
+        for copy in copies(hop):
+            copy.start()
+        return carry
+
+    def end(hop, carry):
+        for copy in copies(hop):
+            copy.wait()
+        return carry
+
+    own_rows = pltpu.make_async_copy(buffer_ref.at[me], tiles_ref.at[me], own_sem.at[0])
+    own_count = pltpu.make_async_copy(counts_ref.at[0], all_ref.at[me], own_sem.at[1])
+    lax.fori_loop(1, devices, begin, 0)
+    own_rows.start()
+    own_count.start()
+    own_rows.wait()
+    own_count.wait()
+    lax.fori_loop(1, devices, end, 0)
+
+
+def route(buffer, counts, devices, seq_count):
+    capacity, width = buffer.shape[1:]
+    lanes = counts.shape[2]
+    return pl.pallas_call(
+        functools.partial(route_kernel, devices, seq_count),
+        in_specs=[pl.BlockSpec(memory_space=pl.ANY)] * 2,
+        out_specs=[pl.BlockSpec(memory_space=pl.ANY)] * 2,
+        out_shape=(
+            jax.ShapeDtypeStruct((devices, capacity, width), BF16),
+            jax.ShapeDtypeStruct((devices, 1, lanes), jnp.int32),
+        ),
+        scratch_shapes=[pltpu.SemaphoreType.DMA((devices,))] * 4
+        + [pltpu.SemaphoreType.DMA((2,))],
+        compiler_params=pltpu.CompilerParams(collective_id=1, has_side_effects=True),
+        name="route",
+    )(buffer, counts)
+
+
+def write_masks(capacity, seq_count, counts_ref, bias_ref, mask_ref):
+    devices, lanes = counts_ref.shape
+    slots = mask_ref.shape[0]
+    half, quarter = slots // 2, slots // 4
+    slide = lax.axis_index("slide")
+    seq = lax.axis_index("seq")
+    core = lax.rem(seq, 2)
+    chip = lax.rem(seq // 2, 2)
+    base = slide * seq_count + seq - core - 2 * chip
+    members = [
+        base + core + 2 * chip,
+        base + (1 - core) + 2 * chip,
+        base + core + 2 * (1 - chip),
+        base + (1 - core) + 2 * (1 - chip),
+    ]
+    counts = counts_ref[...].astype(F32)
+    lane = lax.broadcasted_iota(jnp.int32, (devices, lanes), 1)
+    columns = [
+        jnp.sum(jnp.where(lane == member, counts, 0.0), axis=1, keepdims=True)
+        for member in members
+    ]
+    sender = lax.broadcasted_iota(jnp.int32, (devices, slots), 0) * capacity
+    index = lax.broadcasted_iota(jnp.int32, (devices, slots), 1)
+
+    def row(position, reached):
+        place = (position - sender).astype(F32)
+        inside = jnp.logical_and(place >= 0.0, place < reached)
+        return (jnp.sum(inside.astype(F32), axis=0, keepdims=True) - 1.0) * (-MASKED)
+
+    bias_ref[0:1, :] = row(original_of(index, quarter), columns[0])
+    within = jnp.where(index >= half, index - half, index)
+    for parity in range(2):
+        reached = jnp.where(index >= half, columns[1], columns[0])
+        bias_ref[1 + parity : 2 + parity, :] = row(
+            original_of(within + parity * half, quarter), reached
+        )
+    for phase in range(4):
+        block = (
+            (index >= quarter).astype(jnp.int32)
+            + (index >= 2 * quarter).astype(jnp.int32)
+            + (index >= 3 * quarter).astype(jnp.int32)
+        )
+        reached = jnp.where(
+            index >= half,
+            jnp.where(index >= 3 * quarter, columns[3], columns[2]),
+            jnp.where(index >= quarter, columns[1], columns[0]),
+        )
+        bias_ref[3 + phase : 4 + phase, :] = row(4 * (index - quarter * block) + phase, reached)
+    bias_ref[7:8, :] = jnp.zeros((1, slots), F32)
+    own = (lax.broadcasted_iota(jnp.int32, (8, lanes), 1) == members[0]).astype(F32)
+    reached = lax.dot_general(
+        own, counts, (((1,), (1,)), ((), ())), preferred_element_type=F32
+    )[0:1, :]
+    place = (
+        lax.broadcasted_iota(jnp.int32, (slots, devices), 0)
+        - lax.broadcasted_iota(jnp.int32, (slots, devices), 1) * capacity
+    ).astype(F32)
+    inside = jnp.logical_and(place >= 0.0, place < reached)
+    mask_ref[...] = (jnp.sum(inside.astype(F32), axis=1, keepdims=True) - 1.0) * (-MASKED)
+
+
+def project_kernel(capacity, seq_count, tiles_ref, gain_ref, counts_ref, weight_ref, out_ref, near_ref, far_ref, normed_ref, bias_ref, mask_ref):
     step = pl.program_id(0)
     slots, width = tiles_ref.shape
     quarter = slots // 4
@@ -87,48 +223,74 @@
             normed_ref[:, start : start + WIDE] = jnp.dot(
                 order, normed[:, start : start + WIDE], preferred_element_type=F32
             ).astype(BF16)
+        write_masks(capacity, seq_count, counts_ref, bias_ref, mask_ref)
 
     value = jnp.dot(normed_ref[...], weight_ref[...], preferred_element_type=F32).astype(BF16)
     out_ref[...] = value
-
-    @pl.when(step >= 3)
-    def _():
-        for j in range(GROUP):
-            cols = slice(j * HEAD, (j + 1) * HEAD)
-            near_ref[:, cols] = value[(j % 2) * half : (j % 2 + 1) * half, cols]
-            begin = QUARTER_OF[j] * quarter
-            far_ref[:, cols] = value[begin : begin + quarter, cols]
-
-
-def project(tiles, gain, weight):
+    for j in range(GROUP):
+        cols = slice(j * HEAD, (j + 1) * HEAD)
+        near_ref[:, cols] = value[(j % 2) * half : (j % 2 + 1) * half, cols]
+        begin = QUARTER_OF[j] * quarter
+        far_ref[:, cols] = value[begin : begin + quarter, cols]
+
+
+def project(tiles, gain, counts, weight, capacity, seq_count):
     slots, width = tiles.shape
-    steps = weight.shape[1] // WIDE
-    tail = lambda i: (0, jnp.maximum(i - steps // 3, 0))
-    return pl.pallas_call(
-        project_kernel,
-        grid=(steps,),
+    steps = width // WIDE
+    whole = lambda i: (0, 0)
+    return pl.pallas_call(
+        functools.partial(project_kernel, capacity, seq_count),
+        grid=(2 * steps,),
         in_specs=[
-            pl.BlockSpec((slots, width), lambda i: (0, 0)),
-            pl.BlockSpec((1, width), lambda i: (0, 0)),
-            pl.BlockSpec((width, WIDE), lambda i: (0, i)),
+            pl.BlockSpec((slots, width), whole),
+            pl.BlockSpec((1, width), whole),
+            pl.BlockSpec(counts.shape, whole),
+            pl.BlockSpec((width, WIDE), lambda i: (0, i + steps)),
         ],
         out_specs=[
             pl.BlockSpec((slots, WIDE), lambda i: (0, i)),
-            pl.BlockSpec((slots // 2, WIDE), tail),
-            pl.BlockSpec((slots // 4, WIDE), tail),
+            pl.BlockSpec((slots // 2, WIDE), lambda i: (0, i)),
+            pl.BlockSpec((slots // 4, WIDE), lambda i: (0, i)),
+            pl.BlockSpec((slots, width), whole),
+            pl.BlockSpec((8, slots), whole),
+            pl.BlockSpec((slots, 1), whole),
         ],
         out_shape=(
-            jax.ShapeDtypeStruct((slots, 3 * width), BF16),
+            jax.ShapeDtypeStruct((slots, 2 * width), BF16),
             jax.ShapeDtypeStruct((slots // 2, 2 * width), BF16),
             jax.ShapeDtypeStruct((slots // 4, 2 * width), BF16),
+            jax.ShapeDtypeStruct((slots, width), BF16),
+            jax.ShapeDtypeStruct((8, slots), F32),
+            jax.ShapeDtypeStruct((slots, 1), F32),
         ),
-        scratch_shapes=[pltpu.VMEM((slots, width), BF16)],
+        compiler_params=params(),
+        name="project",
+    )(tiles, gain.reshape(1, width), counts, weight)
+
+
+def query_kernel(normed_ref, weight_ref, out_ref):
+    out_ref[...] = jnp.dot(
+        normed_ref[...], weight_ref[...], preferred_element_type=F32
+    ).astype(BF16)
+
+
+def project_query(normed, weight):
+    slots, width = normed.shape
+    return pl.pallas_call(
+        query_kernel,
+        grid=(width // WIDE,),
+        in_specs=[
+            pl.BlockSpec((slots, width), lambda i: (0, 0)),
+            pl.BlockSpec((width, WIDE), lambda i: (0, i)),
+        ],
+        out_specs=pl.BlockSpec((slots, WIDE), lambda i: (0, i)),
+        out_shape=jax.ShapeDtypeStruct((slots, width), BF16),
         compiler_params=params(),
         cost_estimate=pl.CostEstimate(
-            flops=2 * slots * width * 3 * width, bytes_accessed=30_000_000, transcendentals=0
+            flops=2 * slots * width * width, bytes_accessed=10_000_000, transcendentals=0
         ),
-        name="project",
-    )(tiles, gain.reshape(1, width), weight)
+        name="project_query",
+    )(normed, weight)
 
 
 def softmax_parts(query, keys, values, bias):
@@ -143,54 +305,7 @@
     return summed, peak, total
 
 
-def near_attention_kernel(q_ref, k_ref, v_ref, bias_ref, summed_ref, stats_ref):
-    slots = q_ref.shape[0]
-    half = slots // 2
-    lanes = lax.broadcasted_iota(jnp.int32, (half, HEAD), 1)
-    bias = bias_ref[0:1, :]
-    for part in range(2):
-        rows = slice(part * half, (part + 1) * half)
-        stats = jnp.zeros((half, HEAD), F32)
-        for j in range(GROUP):
-            cols = slice(j * HEAD, (j + 1) * HEAD)
-            summed, peak, total = softmax_parts(q_ref[rows, cols], k_ref[:, cols], v_ref[:, cols], bias)
-            summed_ref[rows, cols] = summed
-            stats = jnp.where(lanes == 2 * j, peak, jnp.where(lanes == 2 * j + 1, total, stats))
-        stats_ref[rows, :] = stats
-
-
-def near_attention(projected, bias):
-    slots, triple = projected.shape
-    width = triple // 3
-    steps = width // WIDE
-    return pl.pallas_call(
-        near_attention_kernel,
-        grid=(steps,),
-        in_specs=[
-            pl.BlockSpec((slots, WIDE), lambda i: (0, i)),
-            pl.BlockSpec((slots, WIDE), lambda i: (0, i + steps)),
-            pl.BlockSpec((slots, WIDE), lambda i: (0, i + 2 * steps)),
-            pl.BlockSpec(bias.shape, lambda i: (0, 0)),
-        ],
-        out_specs=[
-            pl.BlockSpec((slots, WIDE), lambda i: (0, i)),
-            pl.BlockSpec((slots, HEAD), lambda i: (0, i)),
-        ],
-        out_shape=(
-            jax.ShapeDtypeStruct((slots, width), F32),
-            jax.ShapeDtypeStruct((slots, steps * HEAD), F32),
-        ),
-        compiler_params=params(),
-        cost_estimate=pl.CostEstimate(
-            flops=8 * slots * slots * width,
-            bytes_accessed=14_000_000,
-            transcendentals=4 * slots * slots * HEADS,
-        ),
-        name="near_attention",
-    )(projected, projected, projected, bias)
-
-
-def combine(parts):
+def merge(parts):
     top = parts[0][1]
     for _, peak, _ in parts[1:]:
         top = jnp.maximum(top, peak)
@@ -199,34 +314,104 @@
         factor = jnp.exp2(peak - top)
         above = above + factor * summed
         below = below + factor * total
+    return above, top, below
+
+
+def ratio(above, below):
     return (above * (1.0 / jnp.maximum(below, 1.0))).astype(BF16)
 
 
-def far_attention_kernel(
-    q_ref, k_ref, v_ref, bias_ref, pair_k, pair_v, one_k, one_v, two_k, two_v,
-    summed_ref, stats_ref, mixed_ref,
+def near_attention_kernel(
+    q_ref, k_ref, v_ref, bias_ref, pair_k, pair_v, mixed_ref, summed_ref, stats_ref
 ):
     slots = q_ref.shape[0]
     half, quarter = slots // 2, slots // 4
+    lanes = lax.broadcasted_iota(jnp.int32, (quarter, HEAD), 1)
+    stats = jnp.zeros((quarter, HEAD), F32)
     for j in range(GROUP):
         cols = slice(j * HEAD, (j + 1) * HEAD)
         start = (j % 2) * half
-        begin = QUARTER_OF[j] * quarter
-        inside = begin - start
+        inside = QUARTER_OF[j] * quarter - start
         mine = slice(start, start + half)
-        fourth = slice(begin, begin + quarter)
-        within = slice(inside, inside + quarter)
-
-        def local(rows):
-            return (
-                summed_ref[rows, cols],
-                stats_ref[rows, 2 * j : 2 * j + 1],
-                stats_ref[rows, 2 * j + 1 : 2 * j + 2],
-            )
-
+        other = slice(half - start, 2 * half - start)
+        summed, _, total = softmax_parts(
+            q_ref[other, cols], k_ref[:, cols], v_ref[:, cols], bias_ref[0:1, :]
+        )
+        mixed_ref[other, cols] = ratio(summed, total)
+        one = softmax_parts(q_ref[mine, cols], k_ref[:, cols], v_ref[:, cols], bias_ref[0:1, :])
         keys = jnp.concatenate([k_ref[mine, cols], pair_k[:, cols]], axis=0)
         values = jnp.concatenate([v_ref[mine, cols], pair_v[:, cols]], axis=0)
         two = softmax_parts(q_ref[mine, cols], keys, values, bias_ref[1 + j % 2 : 2 + j % 2, :])
+        above, top, below = merge([one, two])
+        done = quarter - inside
+        mixed_ref[start + done : start + done + quarter, cols] = ratio(
+            above[done : done + quarter], below[done : done + quarter]
+        )
+        summed_ref[:, cols] = above[inside : inside + quarter]
+        stats = jnp.where(
+            lanes == 2 * j,
+            top[inside : inside + quarter],
+            jnp.where(lanes == 2 * j + 1, below[inside : inside + quarter], stats),
+        )
+        begin = start + inside
+        mixed_ref[begin : begin + quarter, cols] = jnp.zeros((quarter, HEAD), BF16)
+    stats_ref[...] = stats
+
+
+def halves(array, steps):
+    rows = array.shape[0]
+    return [
+        pl.BlockSpec((rows, WIDE), lambda i: (0, i)),
+        pl.BlockSpec((rows, WIDE), lambda i: (0, i + steps)),
+    ]
+
+
+def near_attention(query, pairs, bias, pair):
+    slots, width = query.shape
+    quarter = slots // 4
+    steps = width // WIDE
+    return pl.pallas_call(
+        near_attention_kernel,
+        grid=(steps,),
+        in_specs=[
+            pl.BlockSpec((slots, WIDE), lambda i: (0, i)),
+            *halves(pairs, steps),
+            pl.BlockSpec(bias.shape, lambda i: (0, 0)),
+            *halves(pair, steps),
+        ],
+        out_specs=[
+            pl.BlockSpec((slots, WIDE), lambda i: (0, i)),
+            pl.BlockSpec((quarter, WIDE), lambda i: (0, i)),
+            pl.BlockSpec((quarter, HEAD), lambda i: (0, i)),
+        ],
+        out_shape=(
+            jax.ShapeDtypeStruct((slots, width), BF16),
+            jax.ShapeDtypeStruct((quarter, width), F32),
+            jax.ShapeDtypeStruct((quarter, steps * HEAD), F32),
+        ),
+        compiler_params=params(),
+        cost_estimate=pl.CostEstimate(
+            flops=12 * slots * slots * width,
+            bytes_accessed=14_000_000,
+            transcendentals=6 * slots * slots * HEADS,
+        ),
+        name="near_attention",
+    )(query, pairs, pairs, bias, pair, pair)
+
+
+def far_attention_kernel(
+    q_ref, k_ref, v_ref, bias_ref, pair_k, pair_v, one_k, one_v, two_k, two_v,
+    summed_ref, stats_ref, near_ref, mixed_ref,
+):
+    slots = q_ref.shape[0]
+    half, quarter = slots // 2, slots // 4
+    mixed_ref[...] = near_ref[...]
+    for j in range(GROUP):
+        cols = slice(j * HEAD, (j + 1) * HEAD)
+        begin = QUARTER_OF[j] * quarter
+        inside = begin - (j % 2) * half
+        fourth = slice(begin, begin + quarter)
+        within = slice(inside, inside + quarter)
         keys = jnp.concatenate(
             [k_ref[fourth, cols], pair_k[within, cols], one_k[:, cols], two_k[:, cols]], axis=0
         )
@@ -234,47 +419,39 @@
             [v_ref[fourth, cols], pair_v[within, cols], one_v[:, cols], two_v[:, cols]], axis=0
         )
         four = softmax_parts(q_ref[fourth, cols], keys, values, bias_ref[3 + j : 4 + j, :])
-        other = slice(half - start, 2 * half - start)
-        mixed_ref[other, cols] = combine([local(other)])
-        for offset in (0, quarter):
-            rows = slice(start + offset, start + offset + quarter)
-            parts = [local(rows), tuple(x[offset : offset + quarter] for x in two)]
-            if offset == inside:
-                parts.append(four)
-            mixed_ref[rows, cols] = combine(parts)
-
-
-def far_attention(projected, bias, pair, one, two, summed, stats):
-    slots, triple = projected.shape
-    width = triple // 3
+        before = (
+            summed_ref[:, cols],
+            stats_ref[:, 2 * j : 2 * j + 1],
+            stats_ref[:, 2 * j + 1 : 2 * j + 2],
+        )
+        above, _, below = merge([before, four])
+        mixed_ref[fourth, cols] = ratio(above, below)
+
+
+def far_attention(query, pairs, bias, pair, one, two, mixed, summed, stats):
+    slots, width = query.shape
+    quarter = slots // 4
     steps = width // WIDE
-
-    def twice(array):
-        rows = array.shape[0]
-        return [
-            pl.BlockSpec((rows, WIDE), lambda i: (0, i)),
-            pl.BlockSpec((rows, WIDE), lambda i: (0, i + steps)),
-        ]
-
+    block = pl.BlockSpec((slots, WIDE), lambda i: (0, i))
     return pl.pallas_call(
         far_attention_kernel,
         grid=(steps,),
         in_specs=[
-            pl.BlockSpec((slots, WIDE), lambda i: (0, i)),
-            pl.BlockSpec((slots, WIDE), lambda i: (0, i + steps)),
-            pl.BlockSpec((slots, WIDE), lambda i: (0, i + 2 * steps)),
+            block,
+            *halves(pairs, steps),
             pl.BlockSpec(bias.shape, lambda i: (0, 0)),
-            *twice(pair),
-            *twice(one),
-            *twice(two),
-            pl.BlockSpec((slots, WIDE), lambda i: (0, i)),
-            pl.BlockSpec((slots, HEAD), lambda i: (0, i)),
+            *halves(pair, steps),
+            *halves(one, steps),
+            *halves(two, steps),
+            pl.BlockSpec((quarter, WIDE), lambda i: (0, i)),
+            pl.BlockSpec((quarter, HEAD), lambda i: (0, i)),
+            block,
         ],
-        out_specs=pl.BlockSpec((slots, WIDE), lambda i: (0, i)),
+        out_specs=block,
         out_shape=jax.ShapeDtypeStruct((slots, width), BF16),
         compiler_params=params(),
         name="far_attention",
-    )(projected, projected, projected, bias, pair, pair, one, one, two, two, summed, stats)
+    )(query, pairs, pairs, bias, pair, pair, one, one, two, two, summed, stats, mixed)
 
 
 def finish_kernel(mixed_ref, tiles_ref, weight_ref, finding_ref, mask_ref, layer_ref, keys_ref, stats_ref, plain_ref):
@@ -405,33 +582,23 @@
     seq_count = lax.axis_size("seq")
     slots = embeds.shape[0] * 2
     capacity = slots // devices
-    half, quarter = slots // 2, slots // 4
-    buffer, counts = dispatch(destination, embeds, devices, capacity)
-    counts = lax.all_gather(counts[0], ("slide", "seq"))[:, :devices]
-    tiles = lax.all_to_all(buffer, ("slide", "seq"), split_axis=0, concat_axis=0, tiled=True)
-
-    me = lax.axis_index(("slide", "seq"))
-    wanted = (me ^ jnp.arange(4, dtype=jnp.int32))[:, None] == jnp.arange(devices, dtype=jnp.int32)
-    reached = jnp.sum(jnp.where(wanted[:, None, :], counts[None], 0), axis=2)
-    open_slots = jnp.arange(capacity, dtype=jnp.int32)[None, None, :] < reached[:, :, None]
-    bias = jnp.where(open_slots, 0.0, MASKED).astype(F32).reshape(4, slots)
-    mask = bias[0].reshape(slots, 1)
-    phased = bias.reshape(4, quarter, 4).transpose(0, 2, 1)
-    phased = jnp.stack([phased[:, 0], phased[:, 2], phased[:, 1], phased[:, 3]], axis=1)
-    rows = [phased[0].reshape(slots)]
-    for parity in range(2):
-        rows.append(phased[:2, 2 * parity : 2 * parity + 2].reshape(slots))
-    for phase in range(4):
-        rows.append(phased[:, QUARTER_OF[phase]].reshape(slots))
-    rows.append(rows[0])
-    bias = jnp.stack(rows)
-
-    projected, near, far = project(tiles, norm_gain, qkv_weight)
+    padded = -(-capacity // 8) * 8
+    width = embeds.shape[1]
+    buffer, counts = dispatch(destination, embeds, devices, padded)
+    received, counts = route(
+        buffer.reshape(devices, padded, width), counts[None], devices, seq_count
+    )
+    tiles = received[:, :capacity].reshape(slots, width)
+    pairs, near, far, normed, bias, mask = project(
+        tiles, norm_gain, counts[:, 0], qkv_weight, capacity, seq_count
+    )
     one = exchange(far, 2)
     pair = exchange(near, 1)
-    summed, stats = near_attention(projected, bias)
+    query = project_query(normed, qkv_weight)
+    mixed, summed, stats = near_attention(query, pairs, bias, pair)
+    one, mixed = lax.optimization_barrier((one, mixed))
     two = exchange(one, 1)
-    mixed = far_attention(projected, bias, pair, one, two, summed, stats)
+    mixed = far_attention(query, pairs, bias, pair, one, two, mixed, summed, stats)
     layer_out, keys, stats = finish(mixed, tiles, out_weight, finding_queries, mask)
     heat = heat_map(seq_count, stats, keys, finding_queries, mask)
     return (layer_out, heat)

time: 240 us -> 157 us (0.65)
  blocking collectives: 59.9 us -> 0 us
  Pallas kernels: 87.4 us -> 141 us
  waiting for transfers between devices: 55.2 us -> 2.84 us
  local copies, waits for them, and re-layouts: 24.5 us -> 7.28 us
  starting transfers between devices: 7.72 us -> 5.23 us
    all_gather x1 -> x0, blocking collectives: 59.9 us -> none  [shards(): counts = lax.all_gather(counts[0], ('slide', 'seq'))[:, :devices]]
    all_to_all x1 -> x0, waiting for transfers between devices: 55.2 us -> none  [shards(): lax.all_to_all(buffer, ('slide', 'seq'), split_axis=0, concat_axis=0, til...]
    pallas_call x2 -> x4, Pallas kernels: 45.1 us -> 92 us  [the longest x1 56.3 us: route(): pl.pallas_call(functools.partial(route_kernel, devices, seq_count), in_sp...]
    another operation x9 -> x0, local copies, waits for them, and re-layouts: 11.8 us -> none  [the longest x8 10.8 us: shards(): bias = jnp.stack(rows)]
    all_to_all x1 -> x0, starting transfers between devices: 7.3 us -> none  [shards(): lax.all_to_all(buffer, ('slide', 'seq'), split_axis=0, concat_axis=0, til...]
    pallas_call x1, Pallas kernels: 13.1 us -> 18.4 us  [near_attention(): pl.pallas_call(near_attention_kernel, grid=(steps,), in_specs=[pl.BlockSp...]
    ppermute x3, starting transfers between devices: 0.42 us -> 5.23 us  [exchange(): return lax.ppermute(value, 'seq', pairs)]
    lt x4 -> x0, local copies, waits for them, and re-layouts: 3.23 us -> none  [shards(): jnp.arange(capacity, dtype=jnp.int32)[None, None, :] < reached[:, :, None]]
  transfers between devices with their start and end apart: 4 -> 3, of which waited for: 1 -> 1; matrix products, arithmetic and copies ran while one was open for 8% -> 0% of each run, Pallas kernels for 6% -> 17%
where the time goes in v2:
time: 157 us
  Pallas kernels  141 us (90%)
  local copies, waits for them, and re-layouts  7.28 us (5%)
  starting transfers between devices  5.23 us (3%)
  waiting for transfers between devices  2.84 us (2%)
    pallas_call x1, Pallas kernels, route(): pl.pallas_call(functools.partial(route_kernel, devices, seq_count), in_sp...  56.3 us
    pallas_call x1, Pallas kernels, near_attention(): pl.pallas_call(near_attention_kernel, grid=(steps,), in_specs=[pl.BlockSp...  18.4 us
    pallas_call x1, Pallas kernels, project(): pl.pallas_call(functools.partial(project_kernel, capacity, seq_count), gr...  15.8 us
    pallas_call x1, Pallas kernels, finish(): pl.pallas_call(finish_kernel, out_shape=(jax.ShapeDtypeStruct((slots, wid...  13.8 us
    pallas_call x1, Pallas kernels, far_attention(): pl.pallas_call(far_attention_kernel, grid=(steps,), in_specs=[block, *hal...  12.3 us
    pallas_call x1, Pallas kernels, heat_map(): pl.pallas_call(functools.partial(heat_kernel, count, count * slots / HEAD...  12.1 us
    pallas_call x1, Pallas kernels, project_query(): pl.pallas_call(query_kernel, grid=(width // WIDE,), in_specs=[pl.BlockSpe...  7.55 us
    unnamed x8, local copies, waits for them, and re-layouts  5.99 us
  transfers between devices with their start and end apart: 3, of which 1 were waited for; matrix products, arithmetic and copies ran while one was open for 0% of the time, Pallas kernels for 17%

profile of v2, /device:TPU:0, one launch (start us, length us, event | category | flops | bytes accessed | tf_op | source)
XLA Modules:
  0.0 156.7 jit_solution(11917875453070734783)
XLA Ops:
  0.6 1.3 reshape.19.gain_ref
  1.9 1.5 copy.8.col_ref
  3.4 4.3 %dispatch.1 = (bf16[768,1536]{1,0:T(8,128)(2,1)}, s32[1,128]{1,0:T(1,128)}) custom-call(s32[384,1]{1,0:T(8,128)} %copy.8.col_ref, s32[1,384]{1,0:T(1,128)} %bitcast.9, bf16[384,1536]{1,0:T(8,128)(2,1)} %embeds_ref.1), custom_call_target="tpu_custom_call" | custom-call | tf_op jit(solution)/shard_map/dispatch/pallas_call | solution.py:51
  7.7 56.3 %route.1 = (bf16[32,24,1536]{2,1,0:T(8,128)(2,1)}, s32[32,1,128]{2,1,0:T(1,128)}) custom-call(bf16[32,24,1536]{2,1,0:T(8,128)(2,1)} %bitcast.7, s32[1,1,128]{2,1,0:T(1,128)} %bitcast.10), custom_call_target="tpu_custom_call" | custom-call | tf_op jit(solution)/shard_map/route/pallas_call | solution.py:132
  64.1 15.8 %project.1 = (bf16[768,3072]{1,0:T(8,128)(2,1)}, bf16[384,3072]{1,0:T(8,128)(2,1)}, bf16[192,3072]{1,0:T(8,128)(2,1)}, bf16[768,1536]{1,0:T(8,128)(2,1)}, f32[8,768]{1,0:T(8,128)}, /*index=5*/f32[768,1]{1,0:T(8,128)}) custom-call(bf16[768,1536]{1,0:T(8,128)(2,1)} %bitcast.5, f32[1,1536]{1,0:T(1,128)} %reshape.19.gain_ref, s32[32,128]{1,0:T(8,128)} %bitcast.8, ...), custom_call_target="tpu_custom_call" | custom-call | tf_op jit(solution)/shard_map/project/pallas_call | solution.py:241
  79.9 1.5 collective-permute-start
  81.4 3.7 %collective-permute-start.1 = (bf16[192,3072]{1,0:T(8,128)(2,1)}, bf16[192,3072]{1,0:T(8,128)(2,1)S(1)}, u32[]{:S(2)}, u32[]{:S(2)}) collective-permute-start(bf16[192,3072]{1,0:T(8,128)(2,1)} %get-tuple-element.28), channel_id=1, source_target_pairs={{0,2},{1,3},{2,0},{3,1},{4,6},{5,7},{6,4},{7,5},{8,10},{9,11},{10,... | collective-permute-start | bytes 3538952 | tf_op jit(solution)/shard_map/ppermute | solution.py:577
  85.1 7.5 %project_query.1.q_ref = bf16[768,1536]{1,0:T(8,128)(2,1)} custom-call(bf16[768,1536]{1,0:T(8,128)(2,1)} %get-tuple-element.24.normed_ref, bf16[1536,4608]{1,0:T(8,128)(2,1)} %weight_ref.4), custom_call_target="tpu_custom_call" | custom-call | flops 3623878656 | bytes 10000000 | tf_op jit(solution)/shard_map/project_query/pallas_call | solution.py:279
  92.6 0.0 collective-permute-done.pair_k.pair_v
  92.6 0.0 copy-start
  92.6 1.4 copy-done
  94.0 18.4 %near_attention.1 = (bf16[768,1536]{1,0:T(8,128)(2,1)}, f32[192,1536]{1,0:T(8,128)}, f32[192,384]{1,0:T(8,128)}) custom-call(bf16[768,1536]{1,0:T(8,128)(2,1)} %project_query.1.q_ref, bf16[768,3072]{1,0:T(8,128)(2,1)} %get-tuple-element.25.k_ref.v_ref, bf16[768,3072]{1,0:T(8,128)(2,1)} %get-tuple-element.25.k_ref.v_ref, ...), custom_call_target="tpu_custom_call" | custom-call | flops 10871635968 | bytes 14000000 | tf_op jit(solution)/shard_map/near_attention/pallas_call | solution.py:373
  112.4 0.0 collective-permute-done.1.one_k.one_v
  112.4 0.0 copy-start.1
  112.4 0.1 collective-permute-start.2
  112.5 2.8 %collective-permute-done.2.two_k.two_v = bf16[192,3072]{1,0:T(8,128)(2,1)S(1)} collective-permute-done((bf16[192,3072]{1,0:T(8,128)(2,1)S(1)}, bf16[192,3072]{1,0:T(8,128)(2,1)S(1)}, u32[]{:S(2)}, u32[]{:S(2)}) %collective-permute-start.2) | collective-permute-done | bytes 1179680 | tf_op jit(solution)/shard_map/ppermute | solution.py:577
  115.4 0.0 copy-start.2
  115.4 0.0 copy-done.1
  115.4 1.0 copy-done.2
  116.4 12.3 %far_attention.1.mixed_ref = bf16[768,1536]{1,0:T(8,128)(2,1)} custom-call(bf16[768,1536]{1,0:T(8,128)(2,1)} %project_query.1.q_ref, bf16[768,3072]{1,0:T(8,128)(2,1)} %get-tuple-element.25.k_ref.v_ref, bf16[768,3072]{1,0:T(8,128)(2,1)} %get-tuple-element.25.k_ref.v_ref, f32[8,768]{1,0:T(8,128)} %get-tuple-element.26.bias_ref, bf16[384,3072]{1,0:T(8,128)(2,1)} %copy-done, ...), custom_call_target="tpu_custom_call" | custom-call | tf_op jit(solution)/shard_map/far_attention/pallas_call | solution.py:436
  128.7 13.8 %finish.1 = (bf16[768,1536]{1,0:T(8,128)(2,1)}, bf16[768,1536]{1,0:T(8,128)(2,1)}, f32[24,256]{1,0:T(8,128)}) custom-call(bf16[768,1536]{1,0:T(8,128)(2,1)} %far_attention.1.mixed_ref, bf16[768,1536]{1,0:T(8,128)(2,1)} %bitcast.6, bf16[1536,1536]{1,0:T(8,128)(2,1)} %weight_ref.5, bf16[256,1536]{1,0:T(8,128)(2,1)} %finding_ref.3, ...), custom_call_target="tpu_custom_call" | custom-call | tf_op jit(solution)/shard_map/finish/pallas_call | solution.py:494
  142.5 12.1 %heat_map.1 = f32[768,256]{1,0:T(8,128)} custom-call(f32[24,256]{1,0:T(8,128)} %get-tuple-element.36.stats_ref, bf16[768,1536]{1,0:T(8,128)(2,1)} %get-tuple-element.37.keys_ref, bf16[256,1536]{1,0:T(8,128)(2,1)} %finding_ref.3, f32[768,1]{1,0:T(8,128)} %get-tuple-element.34.mask_ref), custom_call_target="tpu_custom_call" | custom-call | tf_op jit(solution)/shard_map/heat_map/pallas_call | solution.py:560
  154.6 2.1 %copy.10 = f32[768,256]{1,0:T(8,128)} copy(f32[768,256]{1,0:T(8,128)} %heat_map.1) | data formatting | bytes 1572864
Async XLA Ops:
  79.9 12.7 %collective-permute-start = (bf16[384,3072]{1,0:T(8,128)(2,1)}, bf16[384,3072]{1,0:T(8,128)(2,1)S(1)}, u32[]{:S(2)}, u32[]{:S(2)}) collective-permute-start(bf16[384,3072]{1,0:T(8,128)(2,1)} %get-tuple-element.27), channel_id=1, source_target_pairs={{0,1},{1,0},{2,3},{3,2},{4,5},{5,4},{6,7},{7,6},{8,9},{9,8},{10,11... | collective-permute-start | bytes 7077896 | tf_op jit(solution)/shard_map/ppermute | solution.py:577
  81.4 31.0 %collective-permute-start.1 = (bf16[192,3072]{1,0:T(8,128)(2,1)}, bf16[192,3072]{1,0:T(8,128)(2,1)S(1)}, u32[]{:S(2)}, u32[]{:S(2)}) collective-permute-start(bf16[192,3072]{1,0:T(8,128)(2,1)} %get-tuple-element.28), channel_id=1, source_target_pairs={{0,2},{1,3},{2,0},{3,1},{4,6},{5,7},{6,4},{7,5},{8,10},{9,11},{10,... | collective-permute-start | bytes 3538952 | tf_op jit(solution)/shard_map/ppermute | solution.py:577
  92.6 1.4 copy-start
  112.4 2.9 %copy-start.1 = (bf16[192,3072]{1,0:T(8,128)(2,1)}, bf16[192,3072]{1,0:T(8,128)(2,1)S(1)}, u32[]{:S(2)}) copy-start(bf16[192,3072]{1,0:T(8,128)(2,1)S(1)} %collective-permute-done.1.one_k.one_v) | copy-start | bytes 3538948
  112.4 2.9 %collective-permute-start.2 = (bf16[192,3072]{1,0:T(8,128)(2,1)S(1)}, bf16[192,3072]{1,0:T(8,128)(2,1)S(1)}, u32[]{:S(2)}, u32[]{:S(2)}) collective-permute-start(bf16[192,3072]{1,0:T(8,128)(2,1)S(1)} %collective-permute-done.1.one_k.one_v), channel_id=1, source_target_pairs={{0,1},{1,0},{2,3},{3,2},{4,5},{5,4},{6,7},{7,6},{8,9},{9,8},{10,11... | collective-permute-start | bytes 3538952 | tf_op jit(solution)/shard_map/ppermute | solution.py:577
  115.4 1.0 copy-start.2

commit v3 on v2

--- a/solution.py
+++ b/solution.py
@@ -19,17 +19,18 @@
 BF16 = jnp.bfloat16
 QUARTER_OF = (0, 2, 1, 3)
 VMEM_LIMIT = 56 * 1024 * 1024
-
-
-def params(**more):
-    return pltpu.CompilerParams(vmem_limit_bytes=VMEM_LIMIT, **more)
-
-
-def dispatch_kernel(capacity, col_ref, row_ref, embeds_ref, buffer_ref, counts_ref):
+SMALL_LIMIT = 34 * 1024 * 1024
+
+
+def params(limit=VMEM_LIMIT, **more):
+    return pltpu.CompilerParams(vmem_limit_bytes=limit, **more)
+
+
+def dispatch_kernel(capacity, row_ref, embeds_ref, buffer_ref, counts_ref):
     rows = embeds_ref.shape[0]
     slots = buffer_ref.shape[0]
-    col = col_ref[...]
     row = row_ref[...]
+    col = jnp.transpose(jnp.broadcast_to(row.astype(F32), (128, rows)))[:, 0:1].astype(jnp.int32)
     first = lax.broadcasted_iota(jnp.int32, (rows, rows), 0)
     second = lax.broadcasted_iota(jnp.int32, (rows, rows), 1)
     same = jnp.logical_and(col == row, first < second)
@@ -56,7 +57,7 @@
         ),
         compiler_params=params(),
         name="dispatch",
-    )(destination, destination.reshape(1, rows), embeds)
+    )(destination.reshape(1, rows), embeds)
 
 
 def original_of(index, quarter):
@@ -322,7 +323,7 @@
 
 
 def near_attention_kernel(
-    q_ref, k_ref, v_ref, bias_ref, pair_k, pair_v, mixed_ref, summed_ref, stats_ref
+    q_ref, k_ref, v_ref, bias_ref, pair_k, pair_v, mixed_ref, summed_ref, stats_ref, query_ref
 ):
     slots = q_ref.shape[0]
     half, quarter = slots // 2, slots // 4
@@ -347,14 +348,17 @@
         mixed_ref[start + done : start + done + quarter, cols] = ratio(
             above[done : done + quarter], below[done : done + quarter]
         )
-        summed_ref[:, cols] = above[inside : inside + quarter]
-        stats = jnp.where(
-            lanes == 2 * j,
-            top[inside : inside + quarter],
-            jnp.where(lanes == 2 * j + 1, below[inside : inside + quarter], stats),
-        )
         begin = start + inside
-        mixed_ref[begin : begin + quarter, cols] = jnp.zeros((quarter, HEAD), BF16)
+        fourth = slice(begin, begin + quarter)
+        within = slice(inside, inside + quarter)
+        keys = jnp.concatenate([k_ref[fourth, cols], pair_k[within, cols]], axis=0)
+        values = jnp.concatenate([v_ref[fourth, cols], pair_v[within, cols]], axis=0)
+        four = softmax_parts(q_ref[fourth, cols], keys, values, bias_ref[3 + j : 4 + j, :half])
+        above, top, below = merge([(above[within], top[within], below[within]), four])
+        summed_ref[:, cols] = above
+        stats = jnp.where(lanes == 2 * j, top, jnp.where(lanes == 2 * j + 1, below, stats))
+        query_ref[:, cols] = q_ref[fourth, cols]
+        mixed_ref[fourth, cols] = jnp.zeros((quarter, HEAD), BF16)
     stats_ref[...] = stats
 
 
@@ -383,13 +387,15 @@
             pl.BlockSpec((slots, WIDE), lambda i: (0, i)),
             pl.BlockSpec((quarter, WIDE), lambda i: (0, i)),
             pl.BlockSpec((quarter, HEAD), lambda i: (0, i)),
+            pl.BlockSpec((quarter, WIDE), lambda i: (0, i)),
         ],
         out_shape=(
             jax.ShapeDtypeStruct((slots, width), BF16),
             jax.ShapeDtypeStruct((quarter, width), F32),
             jax.ShapeDtypeStruct((quarter, steps * HEAD), F32),
+            jax.ShapeDtypeStruct((quarter, width), BF16),
         ),
-        compiler_params=params(),
+        compiler_params=params(SMALL_LIMIT),
         cost_estimate=pl.CostEstimate(
             flops=12 * slots * slots * width,
             bytes_accessed=14_000_000,
@@ -400,69 +406,64 @@
 
 
 def far_attention_kernel(
-    q_ref, k_ref, v_ref, bias_ref, pair_k, pair_v, one_k, one_v, two_k, two_v,
-    summed_ref, stats_ref, near_ref, mixed_ref,
+    q_ref, bias_ref, one_k, one_v, two_k, two_v, summed_ref, stats_ref, mixed_ref
 ):
-    slots = q_ref.shape[0]
-    half, quarter = slots // 2, slots // 4
-    mixed_ref[...] = near_ref[...]
+    half = bias_ref.shape[1] // 2
     for j in range(GROUP):
         cols = slice(j * HEAD, (j + 1) * HEAD)
-        begin = QUARTER_OF[j] * quarter
-        inside = begin - (j % 2) * half
-        fourth = slice(begin, begin + quarter)
-        within = slice(inside, inside + quarter)
-        keys = jnp.concatenate(
-            [k_ref[fourth, cols], pair_k[within, cols], one_k[:, cols], two_k[:, cols]], axis=0
-        )
-        values = jnp.concatenate(
-            [v_ref[fourth, cols], pair_v[within, cols], one_v[:, cols], two_v[:, cols]], axis=0
-        )
-        four = softmax_parts(q_ref[fourth, cols], keys, values, bias_ref[3 + j : 4 + j, :])
+        keys = jnp.concatenate([one_k[:, cols], two_k[:, cols]], axis=0)
+        values = jnp.concatenate([one_v[:, cols], two_v[:, cols]], axis=0)
+        four = softmax_parts(q_ref[:, cols], keys, values, bias_ref[3 + j : 4 + j, half:])
         before = (
             summed_ref[:, cols],
             stats_ref[:, 2 * j : 2 * j + 1],
             stats_ref[:, 2 * j + 1 : 2 * j + 2],
         )
         above, _, below = merge([before, four])
-        mixed_ref[fourth, cols] = ratio(above, below)
-
-
-def far_attention(query, pairs, bias, pair, one, two, mixed, summed, stats):
-    slots, width = query.shape
-    quarter = slots // 4
+        mixed_ref[:, cols] = ratio(above, below)
+
+
+def far_attention(query, bias, one, two, summed, stats):
+    quarter, width = query.shape
     steps = width // WIDE
-    block = pl.BlockSpec((slots, WIDE), lambda i: (0, i))
+    block = pl.BlockSpec((quarter, WIDE), lambda i: (0, i))
     return pl.pallas_call(
         far_attention_kernel,
         grid=(steps,),
         in_specs=[
             block,
-            *halves(pairs, steps),
             pl.BlockSpec(bias.shape, lambda i: (0, 0)),
-            *halves(pair, steps),
             *halves(one, steps),
             *halves(two, steps),
-            pl.BlockSpec((quarter, WIDE), lambda i: (0, i)),
+            block,
             pl.BlockSpec((quarter, HEAD), lambda i: (0, i)),
-            block,
         ],
         out_specs=block,
-        out_shape=jax.ShapeDtypeStruct((slots, width), BF16),
-        compiler_params=params(),
+        out_shape=jax.ShapeDtypeStruct((quarter, width), BF16),
+        compiler_params=params(SMALL_LIMIT),
         name="far_attention",
-    )(query, pairs, pairs, bias, pair, pair, one, one, two, two, summed, stats, mixed)
-
-
-def finish_kernel(mixed_ref, tiles_ref, weight_ref, finding_ref, mask_ref, layer_ref, keys_ref, stats_ref, plain_ref):
+    )(query, bias, one, one, two, two, summed, stats)
+
+
+def finish_kernel(mixed_ref, last_ref, tiles_ref, weight_ref, finding_ref, mask_ref, layer_ref, keys_ref, stats_ref, plain_ref):
     slots, width = tiles_ref.shape
     quarter = slots // 4
     position = lax.broadcasted_iota(jnp.int32, (slots, slots), 0)
     index = lax.broadcasted_iota(jnp.int32, (slots, slots), 1)
     order = (original_of(index, quarter) == position).astype(F32).astype(BF16)
     for start in range(0, width, WIDE):
+        heads = []
+        for j in range(GROUP):
+            cols = slice(start + j * HEAD, start + (j + 1) * HEAD)
+            begin = QUARTER_OF[j] * quarter
+            pieces = [last_ref[:, cols]]
+            if begin > 0:
+                pieces.insert(0, mixed_ref[:begin, cols])
+            if begin + quarter < slots:
+                pieces.append(mixed_ref[begin + quarter :, cols])
+            heads.append(jnp.concatenate(pieces, axis=0))
         plain_ref[:, start : start + WIDE] = jnp.dot(
-            order, mixed_ref[:, start : start + WIDE], preferred_element_type=F32
+            order, jnp.concatenate(heads, axis=1), preferred_element_type=F32
         ).astype(BF16)
     square = jnp.zeros((slots, 1), F32)
     for start in range(0, width, WIDE):
@@ -489,7 +490,7 @@
         )
 
 
-def finish(mixed, tiles, weight, finding, mask):
+def finish(mixed, last, tiles, weight, finding, mask):
     slots, width = tiles.shape
     return pl.pallas_call(
         finish_kernel,
@@ -499,12 +500,12 @@
             jax.ShapeDtypeStruct((2 * HEADS, finding.shape[0]), F32),
         ),
         scratch_shapes=[pltpu.VMEM((slots, width), BF16)],
-        compiler_params=params(),
+        compiler_params=params(SMALL_LIMIT),
         name="finish",
-    )(mixed, tiles, weight, finding, mask)
-
-
-def heat_kernel(count, scale, stats_ref, keys_ref, finding_ref, mask_ref, heat_ref, held, send_sem, recv_sem):
+    )(mixed, last, tiles, weight, finding, mask)
+
+
+def heat_kernel(count, scale, stats_ref, keys_ref, finding_ref, mask_ref, heat_ref, held, kept, send_sem, recv_sem):
     slide = lax.axis_index("slide")
     me = lax.axis_index("seq")
     barrier = pltpu.get_barrier_semaphore()
@@ -527,6 +528,14 @@
         )
         copy.start()
         copies.append(copy)
+    mask = mask_ref[...]
+    for h in range(HEADS):
+        cols = slice(h * HEAD, (h + 1) * HEAD)
+        scores = lax.dot_general(
+            keys_ref[:, cols], finding_ref[:, cols], (((1,), (1,)), ((), ())),
+            preferred_element_type=F32,
+        )
+        kept[h] = jnp.exp2(scores * FACTOR + mask - stats_ref[h : h + 1, :])
     for copy in copies:
         copy.wait()
     everything = [stats_ref[...]] + [held[hop] for hop in range(1, count)]
@@ -536,21 +545,14 @@
     totals = jnp.zeros_like(peaks)
     for part in everything:
         totals = totals + part[HEADS:] * jnp.exp2(part[:HEADS] - peaks)
-    factors = scale / totals
+    factors = jnp.exp2(everything[0][:HEADS] - peaks) * (scale / totals)
     slots = keys_ref.shape[0]
-    chunk = slots // 2
+    chunk = 64
     for start in range(0, slots, chunk):
         rows = slice(start, start + chunk)
-        mask = mask_ref[rows, :]
-        total = jnp.zeros((chunk, finding_ref.shape[0]), F32)
-        for h in range(HEADS):
-            cols = slice(h * HEAD, (h + 1) * HEAD)
-            scores = lax.dot_general(
-                keys_ref[rows, cols], finding_ref[:, cols], (((1,), (1,)), ((), ())),
-                preferred_element_type=F32,
-            )
-            scores = scores * FACTOR + mask
-            total = total + jnp.exp2(scores - peaks[h : h + 1]) * factors[h : h + 1]
+        total = kept[0, rows, :] * factors[0:1]
+        for h in range(1, HEADS):
+            total = total + kept[h, rows, :] * factors[h : h + 1]
         heat_ref[rows, :] = total
 
 
@@ -564,10 +566,11 @@
         out_shape=jax.ShapeDtypeStruct((slots, finds), F32),
         scratch_shapes=[
             pltpu.VMEM((count, 2 * HEADS, finds), F32),
+            pltpu.VMEM((HEADS, slots, finds), F32),
             pltpu.SemaphoreType.DMA((count,)),
             pltpu.SemaphoreType.DMA((count,)),
         ],
-        compiler_params=params(collective_id=0, has_side_effects=True),
+        compiler_params=params(SMALL_LIMIT, collective_id=0, has_side_effects=True),
         name="heat_map",
     )(stats, keys, finding, mask)
 
@@ -595,11 +598,11 @@
     one = exchange(far, 2)
     pair = exchange(near, 1)
     query = project_query(normed, qkv_weight)
-    mixed, summed, stats = near_attention(query, pairs, bias, pair)
+    mixed, summed, stats, quarter_query = near_attention(query, pairs, bias, pair)
     one, mixed = lax.optimization_barrier((one, mixed))
     two = exchange(one, 1)
-    mixed = far_attention(query, pairs, bias, pair, one, two, mixed, summed, stats)
-    layer_out, keys, stats = finish(mixed, tiles, out_weight, finding_queries, mask)
+    last = far_attention(quarter_query, bias, one, two, summed, stats)
+    layer_out, keys, stats = finish(mixed, last, tiles, out_weight, finding_queries, mask)
     heat = heat_map(seq_count, stats, keys, finding_queries, mask)
     return (layer_out, heat)
 

time: 157 us -> 142 us (0.904)
  Pallas kernels: 141 us -> 128 us
  local copies, waits for them, and re-layouts: 7.28 us -> 3.86 us
    pallas_call x1, Pallas kernels: 12.1 us -> 7.06 us  [heat_map(): pl.pallas_call(functools.partial(heat_kernel, count, count * slots / HEAD...]
    pallas_call x1, Pallas kernels: 13.8 us -> 9.11 us  [finish(): pl.pallas_call(finish_kernel, out_shape=(jax.ShapeDtypeStruct((slots, wid...]
    pallas_call x1, Pallas kernels: 12.3 us -> 7.99 us  [far_attention(): pl.pallas_call(far_attention_kernel, grid=(steps,), in_specs=[block, pl.B...]
    unnamed x8 -> x17, local copies, waits for them, and re-layouts: 5.99 us -> 2.57 us
  transfers between devices with their start and end apart: 3 -> 3, of which waited for: 1 -> 1; matrix products, arithmetic and copies ran while one was open for 0% -> 0% of each run, Pallas kernels for 17% -> 19%
where the time goes in v3:
time: 142 us; the launch traced here: 141 us
  Pallas kernels  128 us (90%)
  starting transfers between devices  5.22 us (4%)
  local copies, waits for them, and re-layouts  3.86 us (3%)
  waiting for transfers between devices  2.84 us (2%)
    pallas_call x1, Pallas kernels, route(): pl.pallas_call(functools.partial(route_kernel, devices, seq_count), in_sp...  56.3 us
    pallas_call x1, Pallas kernels, near_attention(): pl.pallas_call(near_attention_kernel, grid=(steps,), in_specs=[pl.BlockSp...  19.5 us
    pallas_call x1, Pallas kernels, project(): pl.pallas_call(functools.partial(project_kernel, capacity, seq_count), gr...  15.8 us
    pallas_call x1, Pallas kernels, finish(): pl.pallas_call(finish_kernel, out_shape=(jax.ShapeDtypeStruct((slots, wid...  9.11 us
    pallas_call x1, Pallas kernels, far_attention(): pl.pallas_call(far_attention_kernel, grid=(steps,), in_specs=[block, pl.B...  7.99 us
    pallas_call x1, Pallas kernels, project_query(): pl.pallas_call(query_kernel, grid=(width // WIDE,), in_specs=[pl.BlockSpe...  7.7 us
    pallas_call x1, Pallas kernels, heat_map(): pl.pallas_call(functools.partial(heat_kernel, count, count * slots / HEAD...  7.06 us
    ppermute x3, starting transfers between devices, exchange(): return lax.ppermute(value, 'seq', pairs)  5.22 us
  transfers between devices with their start and end apart: 3, of which 1 were waited for; matrix products, arithmetic and copies ran while one was open for 0% of the time, Pallas kernels for 19%

profile of v3, /device:TPU:0, one launch (start us, length us, event | category | flops | bytes accessed | tf_op | source)
XLA Modules:
  0.0 140.5 jit_solution(16714182028595158346)
XLA Ops:
  0.6 1.3 reshape.19.gain_ref
  1.9 4.4 %dispatch.1 = (bf16[768,1536]{1,0:T(8,128)(2,1)}, s32[1,128]{1,0:T(1,128)}) custom-call(s32[1,384]{1,0:T(1,128)} %bitcast.11, bf16[384,1536]{1,0:T(8,128)(2,1)} %embeds_ref.1), custom_call_target="tpu_custom_call" | custom-call | tf_op jit(solution)/shard_map/dispatch/pallas_call | solution.py:52
  6.3 56.3 %route.1 = (bf16[32,24,1536]{2,1,0:T(8,128)(2,1)}, s32[32,1,128]{2,1,0:T(1,128)}) custom-call(bf16[32,24,1536]{2,1,0:T(8,128)(2,1)} %bitcast.9, s32[1,1,128]{2,1,0:T(1,128)} %bitcast.12), custom_call_target="tpu_custom_call" | custom-call | tf_op jit(solution)/shard_map/route/pallas_call | solution.py:133
  62.6 15.8 %project.1 = (bf16[768,3072]{1,0:T(8,128)(2,1)}, bf16[384,3072]{1,0:T(8,128)(2,1)}, bf16[192,3072]{1,0:T(8,128)(2,1)}, bf16[768,1536]{1,0:T(8,128)(2,1)}, f32[8,768]{1,0:T(8,128)}, /*index=5*/f32[768,1]{1,0:T(8,128)}) custom-call(bf16[768,1536]{1,0:T(8,128)(2,1)} %bitcast.5, f32[1,1536]{1,0:T(1,128)} %reshape.19.gain_ref, s32[32,128]{1,0:T(8,128)} %bitcast.10, ...), custom_call_target="tpu_custom_call" | custom-call | tf_op jit(solution)/shard_map/project/pallas_call | solution.py:242
  78.4 1.5 %collective-permute-start.1 = (bf16[384,3072]{1,0:T(8,128)(2,1)}, bf16[384,3072]{1,0:T(8,128)(2,1)}, u32[]{:S(2)}, u32[]{:S(2)}) collective-permute-start(bf16[384,3072]{1,0:T(8,128)(2,1)} %get-tuple-element.29), channel_id=1, source_target_pairs={{0,1},{1,0},{2,3},{3,2},{4,5},{5,4},{6,7},{7,6},{8,9},{9,8},{10,11... | collective-permute-start | bytes 7077896 | tf_op jit(solution)/shard_map/ppermute | solution.py:580
  79.9 3.7 %collective-permute-start = (bf16[192,3072]{1,0:T(8,128)(2,1)}, bf16[192,3072]{1,0:T(8,128)(2,1)S(1)}, u32[]{:S(2)}, u32[]{:S(2)}) collective-permute-start(bf16[192,3072]{1,0:T(8,128)(2,1)} %get-tuple-element.25), channel_id=1, source_target_pairs={{0,2},{1,3},{2,0},{3,1},{4,6},{5,7},{6,4},{7,5},{8,10},{9,11},{10,... | collective-permute-start | bytes 3538952 | tf_op jit(solution)/shard_map/ppermute | solution.py:580
  83.6 0.0 copy-start.4
  83.6 0.0 copy-start.5
  83.6 0.0 slice-start
  83.6 7.7 %project_query.1.q_ref = bf16[768,1536]{1,0:T(8,128)(2,1)} custom-call(bf16[768,1536]{1,0:T(8,128)(2,1)} %get-tuple-element.26.normed_ref, bf16[1536,4608]{1,0:T(8,128)(2,1)} %weight_ref.4), custom_call_target="tpu_custom_call" | custom-call | flops 3623878656 | bytes 10000000 | tf_op jit(solution)/shard_map/project_query/pallas_call | solution.py:280
  91.3 0.0 collective-permute-done.1.pair_k.pair_v
  91.3 0.0 copy-done.4
  91.3 0.0 copy-done.5
  91.3 0.0 copy-start.2
  91.3 1.7 %copy-done.2 = bf16[768,1536]{1,0:T(8,128)(2,1)S(1)} copy-done((bf16[768,1536]{1,0:T(8,128)(2,1)S(1)}, bf16[768,1536]{1,0:T(8,128)(2,1)}, u32[]{:S(2)}) %copy-start.2) | copy-done | bytes 2359320
  93.0 0.0 slice-start.1
  93.0 19.5 %near_attention.1 = (bf16[768,1536]{1,0:T(8,128)(2,1)S(1)}, f32[192,1536]{1,0:T(8,128)S(1)}, f32[192,384]{1,0:T(8,128)S(1)}, bf16[192,1536]{1,0:T(8,128)(2,1)S(1)}) custom-call(bf16[768,1536]{1,0:T(8,128)(2,1)S(1)} %copy-done.2, bf16[768,3072]{1,0:T(8,128)(2,1)S(1)} %copy-done.5, bf16[768,3072]{1,0:T(8,128)(2,1)S(1)} %copy-done.5, f32[8,768]{1,0:T(8,128)S(1)} %copy-done.4, ...), custom_call_target="tpu_custom_call" | custom-call | flops 10871635968 | bytes 14000000 | tf_op jit(solution)/shard_map/near_attention/pallas_call | solution.py:377
  112.5 0.0 collective-permute-done.one_k.one_v
  112.5 0.1 collective-permute-start.2
  112.6 2.8 %collective-permute-done.2.two_k.two_v = bf16[192,3072]{1,0:T(8,128)(2,1)S(1)} collective-permute-done((bf16[192,3072]{1,0:T(8,128)(2,1)S(1)}, bf16[192,3072]{1,0:T(8,128)(2,1)S(1)}, u32[]{:S(2)}, u32[]{:S(2)}) %collective-permute-start.2) | collective-permute-done | bytes 1179680 | tf_op jit(solution)/shard_map/ppermute | solution.py:580
  115.4 0.0 copy-start
  115.4 0.0 copy-start.1
  115.4 0.0 copy-start.3
  115.4 8.0 %far_attention.1.last_ref = bf16[192,1536]{1,0:T(8,128)(2,1)S(1)} custom-call(bf16[192,1536]{1,0:T(8,128)(2,1)S(1)} %get-tuple-element.32.q_ref, f32[8,768]{1,0:T(8,128)S(1)} %copy-done.4, bf16[192,3072]{1,0:T(8,128)(2,1)S(1)} %collective-permute-done.one_k.one_v, bf16[192,3072]{1,0:T(8,128)(2,1)S(1)} %collective-permute-done.one_k.one_v, ...), custom_call_target="tpu_custom_call" | custom-call | tf_op jit(solution)/shard_map/far_attention/pallas_call | solution.py:430
  123.4 0.0 slice-done
  123.4 0.0 slice-done.1
  123.4 0.0 copy-done
  123.4 0.0 copy-done.1
  123.4 0.0 copy-done.3
  123.5 9.1 %finish.1 = (bf16[768,1536]{1,0:T(8,128)(2,1)}, bf16[768,1536]{1,0:T(8,128)(2,1)S(1)}, f32[24,256]{1,0:T(8,128)S(1)}) custom-call(bf16[768,1536]{1,0:T(8,128)(2,1)S(1)} %get-tuple-element.31.mixed_ref, bf16[192,1536]{1,0:T(8,128)(2,1)S(1)} %far_attention.1.last_ref, bf16[768,1536]{1,0:T(8,128)(2,1)S(1)} %bitcast.6, bf16[1536,1536]{1,0:T(8,128)(2,1)S(1)} %bitcast.8, ...), custom_call_target="tpu_custom_call" | custom-call | tf_op jit(solution)/shard_map/finish/pallas_call | solution.py:495
  132.6 7.1 %heat_map.1 = f32[768,256]{1,0:T(8,128)S(1)} custom-call(f32[24,256]{1,0:T(8,128)S(1)} %get-tuple-element.38.stats_ref, bf16[768,1536]{1,0:T(8,128)(2,1)S(1)} %get-tuple-element.39.keys_ref, bf16[256,1536]{1,0:T(8,128)(2,1)S(1)} %copy-done.1, f32[768,1]{1,0:T(8,128)S(1)} %copy-done.3), custom_call_target="tpu_custom_call" | custom-call | tf_op jit(solution)/shard_map/heat_map/pallas_call | solution.py:562
  139.6 0.9 copy.9
  (1 shorter events, 0.0 us)
Async XLA Ops:
  78.4 12.9 %collective-permute-start.1 = (bf16[384,3072]{1,0:T(8,128)(2,1)}, bf16[384,3072]{1,0:T(8,128)(2,1)}, u32[]{:S(2)}, u32[]{:S(2)}) collective-permute-start(bf16[384,3072]{1,0:T(8,128)(2,1)} %get-tuple-element.29), channel_id=1, source_target_pairs={{0,1},{1,0},{2,3},{3,2},{4,5},{5,4},{6,7},{7,6},{8,9},{9,8},{10,11... | collective-permute-start | bytes 7077896 | tf_op jit(solution)/shard_map/ppermute | solution.py:580
  79.9 32.6 %collective-permute-start = (bf16[192,3072]{1,0:T(8,128)(2,1)}, bf16[192,3072]{1,0:T(8,128)(2,1)S(1)}, u32[]{:S(2)}, u32[]{:S(2)}) collective-permute-start(bf16[192,3072]{1,0:T(8,128)(2,1)} %get-tuple-element.25), channel_id=1, source_target_pairs={{0,2},{1,3},{2,0},{3,1},{4,6},{5,7},{6,4},{7,5},{8,10},{9,11},{10,... | collective-permute-start | bytes 3538952 | tf_op jit(solution)/shard_map/ppermute | solution.py:580
  83.6 7.7 %copy-start.4 = (f32[8,768]{1,0:T(8,128)S(1)}, f32[8,768]{1,0:T(8,128)}, u32[]{:S(2)}) copy-start(f32[8,768]{1,0:T(8,128)} %get-tuple-element.28.bias_ref) | copy-start | bytes 73732
  83.6 7.7 %copy-start.5 = (bf16[768,3072]{1,0:T(8,128)(2,1)S(1)}, bf16[768,3072]{1,0:T(8,128)(2,1)}, u32[]{:S(2)}) copy-start(bf16[768,3072]{1,0:T(8,128)(2,1)} %get-tuple-element.27.k_ref.v_ref) | copy-start | bytes 14155780
  83.6 39.8 %slice-start = ((s8[4718592]{0:T(1024)(128)(4,1)}), s8[524288]{0:T(1024)(128)(4,1)S(1)}, s32[]{:S(2)}) async-start(s8[4718592]{0:T(1024)(128)(4,1)} %bitcast.7), calls=%async_computation | async-start | bytes 1048576
  91.3 1.7 %copy-start.2 = (bf16[768,1536]{1,0:T(8,128)(2,1)S(1)}, bf16[768,1536]{1,0:T(8,128)(2,1)}, u32[]{:S(2)}) copy-start(bf16[768,1536]{1,0:T(8,128)(2,1)} %project_query.1.q_ref) | copy-start | bytes 7077892
  93.0 30.5 %slice-start.1 = ((s8[4718592]{0:T(1024)(128)(4,1)}), s8[4194304]{0:T(1024)(128)(4,1)S(1)}, s32[]{:S(2)}) async-start(s8[4718592]{0:T(1024)(128)(4,1)} %bitcast.7), calls=%async_computation.1 | async-start | bytes 8388608
  112.5 2.9 %collective-permute-start.2 = (bf16[192,3072]{1,0:T(8,128)(2,1)S(1)}, bf16[192,3072]{1,0:T(8,128)(2,1)S(1)}, u32[]{:S(2)}, u32[]{:S(2)}) collective-permute-start(bf16[192,3072]{1,0:T(8,128)(2,1)S(1)} %collective-permute-done.one_k.one_v), channel_id=1, source_target_pairs={{0,1},{1,0},{2,3},{3,2},{4,5},{5,4},{6,7},{7,6},{8,9},{9,8},{10,11... | collective-permute-start | bytes 3538952 | tf_op jit(solution)/shard_map/ppermute | solution.py:580
  115.4 8.0 %copy-start = (bf16[32,24,1536]{2,1,0:T(8,128)(2,1)S(1)}, bf16[32,24,1536]{2,1,0:T(8,128)(2,1)}, u32[]{:S(2)}) copy-start(bf16[32,24,1536]{2,1,0:T(8,128)(2,1)} %get-tuple-element.23) | copy-start | bytes 7077892
  115.4 8.0 %copy-start.1 = (bf16[256,1536]{1,0:T(8,128)(2,1)S(1)}, bf16[256,1536]{1,0:T(8,128)(2,1)}, u32[]{:S(2)}) copy-start(bf16[256,1536]{1,0:T(8,128)(2,1)} %finding_ref.3) | copy-start | bytes 2359300
  115.4 8.0 %copy-start.3 = (f32[768,1]{1,0:T(8,128)S(1)}, f32[768,1]{1,0:T(8,128)}, u32[]{:S(2)}) copy-start(f32[768,1]{1,0:T(8,128)} %get-tuple-element.36.mask_ref) | copy-start | bytes 9220
